TPU v7x, 1024 devices: a whole 4x8x16 slice. The times are simulated.
1024 devices in a mesh: gx: 32 (over x, y), gy: 32 (over z, core).
Axes of the slice: x: 4, y: 8, z: 16, core: 2. Of those that a mesh axis runs over, the one named last changes fastest.
Arguments:
- basis: float32 [32, 512, 256, 128], P(None, 'gx', 'gy'), may hold values from -21 to 21
- classes: int32 [512, 256, 128], P('gx', 'gy'), may hold values from 0 to 7
- ports: int32 [512, 256, 128], P('gx', 'gy'), may hold values from 0 to 8, as said below
- taps: float32 [8, 42], replicated, may hold values from 0.05 to 0.5
- port_gain: float32 [8], replicated, may hold values from 0.5 to 4
Outputs:
- next_block: float32 [8, 512, 256, 128], P(None, 'gx', 'gy')
- projection: float32 [32, 8], replicated
- triangle: float32 [8, 8], replicated
Inputs may be any that keep to these rules, and one draw needn't show every extreme that they name: `ports`: 0 means the cell belongs to no port; p in 1..8 names port p.
All inputs are finite; a program needn't handle non-finite values.
Results may differ from a plain program's by a relative error of at most 0.00029.
Values sent between devices are 32-bit elements; how exact they have to be, the bound alone decides.
No kernel may reach another device: no remote copies, remote signals or barrier semaphores. Data moves between devices by JAX's collectives and lax.ppermute only.
A program may use at most 32 MiB of HBM per device.

v0:
```python
import jax
import jax.numpy as jnp
from jax import lax
from jax.sharding import Mesh
from jax.sharding import PartitionSpec as P

COLS = 8
BLOCKS = 4
REACH = 7
MAT = 8
PORTS = 8
GX_GY = ("gx_0", "gx_1", "gy_0", "gy_1")
GX = ("gx_0", "gx_1")
GY = ("gy_0", "gy_1")


def extended(value, sides, width):
    edges = {}
    for axis, dim in sides:
        devices, length = (lax.axis_size(axis), value.shape[dim])
        up = [(i, (i + 1) % devices) for i in range(devices - 1)]
        last = lax.slice_in_dim(value, length - width, length, axis=dim)
        initial = lax.slice_in_dim(value, 0, width, axis=dim)
        edges[dim] = (
            lax.ppermute(last, axis, up),
            lax.ppermute(initial, axis, [(b, a) for a, b in up]),
        )
    done = []
    for _, dim in sides:
        low, high = edges[dim]
        around = [(width, width) if d in done else (0, 0) for d in range(value.ndim)]
        value = jnp.concatenate([jnp.pad(low, around), value, jnp.pad(high, around)], axis=dim)
        done.append(dim)
    return value


def one_axis_at_a_time(value, axes):
    for axis in axes:
        value = lax.psum(value, axis)
    return value


def apply_taps(image, source, coefs, dim, axis_pos, length):
    for j in range(2 * REACH):
        offset = j - REACH if j < REACH else j - REACH + 1
        shifted = lax.slice_in_dim(source, REACH + offset, REACH + offset + length, axis=axis_pos)
        image = image - coefs[2 * REACH * dim + j][None] * shifted
    return image


def per_device(basis, classes, ports, taps, port_gain):
    highest = lax.Precision.HIGHEST
    size_x, size_y, size_z = classes.shape
    block = basis[(BLOCKS - 1) * COLS :]
    kinds = jnp.arange(MAT, dtype=jnp.int32)
    onehot = (classes[None] == kinds[:, None, None, None]).astype(jnp.float32)
    coefs = jnp.einsum("mt,mxyz->txyz", taps, onehot, precision=highest)
    gains_full = jnp.concatenate([jnp.zeros((1,), jnp.float32), port_gain])
    port_kinds = jnp.arange(PORTS + 1, dtype=jnp.int32)
    port_hot = (ports[None] == port_kinds[:, None, None, None]).astype(jnp.float32)
    gain_cell = jnp.einsum("p,pxyz->xyz", gains_full, port_hot, precision=highest)
    diag = (
        1.0
        + jnp.einsum("m,mxyz->xyz", jnp.sum(taps, axis=1), onehot, precision=highest)
        + gain_cell
    )
    image = diag[None] * block
    z_padded = jnp.pad(block, ((0, 0), (0, 0), (0, 0), (REACH, REACH)))
    padded = extended(block, ((GX, 1), (GY, 2)), REACH)
    image = apply_taps(image, padded[:, :, REACH : REACH + size_y, :], coefs, 0, 1, size_x)
    image = apply_taps(image, padded[:, REACH : REACH + size_x, :, :], coefs, 1, 2, size_y)
    image = apply_taps(image, z_padded, coefs, 2, 3, size_z)
    total = size_x * size_y * size_z * lax.axis_size(GX) * lax.axis_size(GY)
    basis_flat = basis.reshape(BLOCKS * COLS, -1)
    image_flat = image.reshape(COLS, -1)
    local_qw = jnp.dot(basis_flat, image_flat.T, precision=highest)
    local_ww = jnp.dot(image_flat, image_flat.T, precision=highest)
    local_qq = jnp.dot(basis_flat, basis_flat.T, precision=highest)
    sum_qw, sum_ww, sum_qq = (
        one_axis_at_a_time(local_qw, GX_GY),
        one_axis_at_a_time(local_ww, GX_GY),
        one_axis_at_a_time(local_qq, GX_GY),
    )
    projection = sum_qw / total
    cross = jnp.dot(projection.T, projection, precision=highest)
    inner = jnp.dot(sum_qq / total, projection, precision=highest)
    gram = sum_ww / total - 2.0 * cross + jnp.dot(projection.T, inner, precision=highest)
    remainder = image_flat - jnp.dot(projection.T, basis_flat, precision=highest)
    lower = jnp.linalg.cholesky(gram)
    solved = lax.linalg.triangular_solve(lower, remainder, left_side=True, lower=True)
    return (solved.reshape(COLS, size_x, size_y, size_z), projection, lower.T)


def solution(mesh):
    split = Mesh(mesh.devices.reshape(4, 8, 16, 2), ("gx_0", "gx_1", "gy_0", "gy_1"))
    in_specs = (P(None, GX, GY, None), P(GX, GY, None), P(GX, GY, None), P(), P())
    out_specs = (P(None, GX, GY, None), P(), P())
    return jax.shard_map(
        per_device, mesh=split, in_specs=in_specs, out_specs=out_specs, check_vma=False
    )
```

profile of v0, /device:TPU:1, one launch (start us, length us, event | category | flops | bytes accessed | tf_op | source)
XLA Modules:
  0.0 170.3 jit_solution(14435626443365449882)
XLA Ops:
  0.7 2.4 %fusion.116 = (f32[8,16,7,128]{3,2,1,0:T(8,128)}, f32[8,16,7,128]{3,2,1,0:T(8,128)}) fusion(f32[32,16,8,128]{3,2,1,0:T(8,128)} %param.5), kind=kLoop, calls=%fused_computation.187 | loop fusion | bytes 1835008 | tf_op jit(solution)/shard_map/slice | solution.py:22
  3.1 5.4 %collective-permute-start.2 = (f32[8,16,7,128]{3,2,1,0:T(8,128)}, f32[8,16,7,128]{3,2,1,0:T(8,128)S(1)}, u32[]{:S(2)}, u32[]{:S(2)}) collective-permute-start(f32[8,16,7,128]{3,2,1,0:T(8,128)} %get-tuple-element.60), channel_id=1, source_target_pairs={{0,1},{1,2},{2,3},{3,4},{4,5},{5,6},{6,7},{7,8},{8,9},{9,10},{10,1... | collective-permute-start | bytes 1376264 | tf_op jit(solution)/shard_map/ppermute | solution.py:25
  8.5 0.8 fusion.117
  9.3 1.3 collective-permute-start.1
  10.6 4.0 %collective-permute-start = (f32[8,7,8,128]{3,2,1,0:T(8,128)}, f32[8,7,8,128]{3,2,1,0:T(8,128)S(1)}, u32[]{:S(2)}, u32[]{:S(2)}) collective-permute-start(f32[8,7,8,128]{3,2,1,0:T(8,128)} %get-tuple-element.62), channel_id=1, source_target_pairs={{0,32},{32,64},{64,96},{96,128},{128,160},{160,192},{192,224},{224... | collective-permute-start | bytes 688136 | tf_op jit(solution)/shard_map/ppermute | solution.py:25
  14.6 12.5 %collective-permute-start.3 = (f32[8,16,7,128]{3,2,1,0:T(8,128)}, f32[8,16,7,128]{3,2,1,0:T(8,128)}, u32[]{:S(2)}, u32[]{:S(2)}) collective-permute-start(f32[8,16,7,128]{3,2,1,0:T(8,128)} %get-tuple-element.61), channel_id=1, source_target_pairs={{1,0},{2,1},{3,2},{4,3},{5,4},{6,5},{7,6},{8,7},{9,8},{10,9},{11,1... | collective-permute-start | bytes 1376264 | tf_op jit(solution)/shard_map/ppermute | solution.py:26
  27.1 1.4 convolution_bitcast_fusion
  28.6 1.7 %fusion.113 = (f32[1,16,8,128]{3,0,2,1:T(1,128)S(1)}, f32[1,16,8,128]{3,0,2,1:T(1,128)S(1)}, f32[1,16,8,128]{3,0,2,1:T(1,128)S(1)}, f32[1,16,8,128]{3,0,2,1:T(1,...) fusion(f32[42,16,8,128]{3,0,2,1:T(8,128)S(1)} %convolution_bitc, ...), kind=kLoop, calls=%fused_computation.184 | loop fusion | bytes 2490368 | tf_op jit(solution)/shard_map/slice | solution.py:47
  30.3 1.8 %fusion.114 = (f32[1,16,8,128]{3,0,2,1:T(1,128)}, f32[1,16,8,128]{3,0,2,1:T(1,128)}, f32[1,16,8,128]{3,0,2,1:T(1,128)}, f32[1,16,8,128]{3,0,2,1:T(1,128)}, f32[1...) fusion(f32[42,16,8,128]{3,0,2,1:T(8,128)S(1)} %convolution_bitc, ...), kind=kLoop, calls=%fused_computation.185 | loop fusion | bytes 2490368 | tf_op jit(solution)/shard_map/slice | solution.py:47
  32.1 0.9 fusion.115
  33.7 0.7 iota_compare_fusion.2
  34.6 1.4 fusion.13
  35.9 1.3 fusion.109
  37.2 3.4 %fusion.6 = f32[32,32]{1,0:T(8,128)} fusion(f32[32,16,8,128]{3,2,1,0:T(8,128)S(1)} %copy-done.1), kind=kOutput, calls=%fused_computation.38 | convolution fusion | flops 201326592 | bytes 2101248 | tf_op jit(solution)/shard_map/dot_general | solution.py:78
  41.1 1.7 %select_maximum_fusion.1 = (f32[8,30,15,128]{3,2,1,0:T(8,128)S(1)}, f32[8,30,15,128]{3,2,1,0:T(8,128)S(1)}) fusion(f32[8,16,7,128]{3,2,1,0:T(8,128)S(1)} %collective-permute-done.2, f32[8,7,8,128]{3,2,1,0:T(8,128)S(1)} %collective-permute-done.1, f32[8,16,8,128]{3,2,1,0:T(8,128)S(1)} %slice.324, f32[8,7,8,128]{3,2,1,0:T(8,128)S(1)} %collective-permute-done, ...), kind=kLoop, calls=%fused_computation.23 | loop fusion | flops 4608000 | bytes 5586944 | tf_op jit(solution)/shard_map/concatenate | solution.py:32
  43.2 5.5 %fusion.86 = f32[8,16,8,128]{3,2,1,0:T(8,128)S(1)} fusion(f32[8,16,8,128]{3,2,1,0:T(8,128)S(1)} %slice.324, f32[8,30,15,128]{3,2,1,0:T(8,128)S(1)} %get-tuple-element.65, f32[8,30,15,128]{3,2,1,0:T(8,128)S(1)} %get-tuple-element.64, f32[8,7,8,128]{3,2,1,0:T(8,128)S(1)} %collective-permute-done.1, f32[8,7,8,128]{3,2,1,0:T(8,128)S(1)} %collective-permute-done, ...), kind=kLoop, calls=%fused_computation.130 | loop fusion | flops 12976128 | bytes 11665408 | tf_op jit(solution)/shard_map/sub | solution.py:47
  48.7 2.9 %fusion.10 = f32[32,8]{0,1:T(8,128)S(1)} fusion(f32[32,16,8,128]{3,2,1,0:T(8,128)S(1)} %copy-done.1, f32[8,16,8,128]{3,2,1,0:T(8,128)S(1)} %fusion.86), kind=kOutput, calls=%fused_computation.43 | convolution fusion | flops 50331648 | bytes 2622464 | tf_op jit(solution)/shard_map/dot_general | solution.py:76
  51.6 1.3 convolution_bitcast_fusion.1
  52.9 10.9 %all-reduce.5 = (f32[32,8]{0,1:T(8,128)S(1)}, f32[8,8]{0,1:T(8,128)S(1)}, f32[32,32]{1,0:T(8,128)S(1)}) all-reduce(f32[32,8]{0,1:T(8,128)S(1)} %fusion.10, f32[8,8]{0,1:T(8,128)S(1)} %convolution_bitcast_fusion.1, f32[32,32]{1,0:T(8,128)S(1)} %copy-done.39), channel_id=1, replica_groups=mesh['gx_0'=4,'gx_1'=8,'gy_0'=16,'gy_1'=2] {'gx_0'}, use_global_device_ids=true, to_apply=%region_5.6 | all-reduce | flops 1344 | bytes 10752 | tf_op jit(solution)/shard_map/psum | solution.py:39
  63.8 20.2 %all-reduce.4 = (f32[32,8]{0,1:T(8,128)S(1)}, f32[8,8]{0,1:T(8,128)S(1)}, f32[32,32]{1,0:T(8,128)S(1)}) all-reduce(f32[32,8]{0,1:T(8,128)S(1)} %get-tuple-element.12, f32[8,8]{0,1:T(8,128)S(1)} %get-tuple-element.13, f32[32,32]{1,0:T(8,128)S(1)} %get-tuple-element.14), channel_id=1, replica_groups=mesh['gx_0'=4,'gx_1'=8,'gy_0'=16,'gy_1'=2] {'gx_1'}, use_global_device_ids=true, to_apply=%region_6.7 | all-reduce | flops 1344 | bytes 10752 | tf_op jit(solution)/shard_map/psum | solution.py:39
  84.0 49.8 %all-reduce.3 = (f32[32,8]{0,1:T(8,128)S(1)}, f32[8,8]{0,1:T(8,128)S(1)}, f32[32,32]{1,0:T(8,128)S(1)}) all-reduce(f32[32,8]{0,1:T(8,128)S(1)} %get-tuple-element.9, f32[8,8]{0,1:T(8,128)S(1)} %get-tuple-element.10, f32[32,32]{1,0:T(8,128)S(1)} %get-tuple-element.11), channel_id=1, replica_groups=mesh['gx_0'=4,'gx_1'=8,'gy_0'=16,'gy_1'=2] {'gy_0'}, use_global_device_ids=true, to_apply=%region_7.8 | all-reduce | flops 1344 | bytes 10752 | tf_op jit(solution)/shard_map/psum | solution.py:39
  133.8 28.6 %all-reduce.6 = (f32[32,8]{0,1:T(8,128)S(1)}, f32[8,8]{0,1:T(8,128)S(1)}, f32[32,32]{1,0:T(8,128)S(1)}) all-reduce(f32[32,8]{0,1:T(8,128)S(1)} %get-tuple-element.6, f32[8,8]{0,1:T(8,128)S(1)} %get-tuple-element.7, f32[32,32]{1,0:T(8,128)S(1)} %get-tuple-element.8), channel_id=1, replica_groups=mesh['gx_0'=4,'gx_1'=8,'gy_0'=16,'gy_1'=2] {'gy_1'}, use_global_device_ids=true, to_apply=%region_8.9 | all-reduce | flops 1344 | bytes 10752 | tf_op jit(solution)/shard_map/psum | solution.py:39
  165.7 2.4 %convolution_subtract_fusion = f32[8,16384]{1,0:T(8,128)S(1)} fusion(f32[32,8]{0,1:T(8,128)S(1)} %broadcast_multiply_fusion, f32[4,8,128,128]{3,2,1,0:T(8,128)S(1)} %bitcast.111, f32[1,8,128,128]{3,2,1,0:T(8,128)S(1)} %bitcast.112), kind=kOutput, calls=%fused_computation | convolution fusion | flops 50462720 | bytes 3146752 | tf_op jit(solution)/shard_map/dot_general | solution.py:88
  168.8 0.9 copy.17
  (105 shorter events, 5.6 us)
Async XLA Ops:
  0.6 26.5 %copy-start = (f32[8,42]{1,0:T(8,128)S(1)}, f32[8,42]{1,0:T(8,128)}, u32[]{:S(2)}) copy-start(f32[8,42]{1,0:T(8,128)} %param.8) | copy-start | bytes 4036
  0.6 7.8 %copy-start.1 = (f32[32,16,8,128]{3,2,1,0:T(8,128)S(1)}, f32[32,16,8,128]{3,2,1,0:T(8,128)}, u32[]{:S(2)}) copy-start(f32[32,16,8,128]{3,2,1,0:T(8,128)} %param.5) | copy-start | bytes 6291460
  0.7 26.5 %copy-start.37 = (s32[16,8,128]{2,1,0:T(8,128)S(1)}, s32[16,8,128]{2,1,0:T(8,128)}, u32[]{:S(2)}) copy-start(s32[16,8,128]{2,1,0:T(8,128)} %param.6) | copy-start | bytes 196612
  3.1 38.0 %collective-permute-start.2 = (f32[8,16,7,128]{3,2,1,0:T(8,128)}, f32[8,16,7,128]{3,2,1,0:T(8,128)S(1)}, u32[]{:S(2)}, u32[]{:S(2)}) collective-permute-start(f32[8,16,7,128]{3,2,1,0:T(8,128)} %get-tuple-element.60), channel_id=1, source_target_pairs={{0,1},{1,2},{2,3},{3,4},{4,5},{5,6},{6,7},{7,8},{8,9},{9,10},{10,1... | collective-permute-start | bytes 1376264 | tf_op jit(solution)/shard_map/ppermute | solution.py:25
  9.3 31.8 %collective-permute-start.1 = (f32[8,7,8,128]{3,2,1,0:T(8,128)}, f32[8,7,8,128]{3,2,1,0:T(8,128)S(1)}, u32[]{:S(2)}, u32[]{:S(2)}) collective-permute-start(f32[8,7,8,128]{3,2,1,0:T(8,128)} %get-tuple-element.63), channel_id=1, source_target_pairs={{32,0},{64,32},{96,64},{128,96},{160,128},{192,160},{224,192},{256... | collective-permute-start | bytes 688136 | tf_op jit(solution)/shard_map/ppermute | solution.py:26
  10.6 30.5 %collective-permute-start = (f32[8,7,8,128]{3,2,1,0:T(8,128)}, f32[8,7,8,128]{3,2,1,0:T(8,128)S(1)}, u32[]{:S(2)}, u32[]{:S(2)}) collective-permute-start(f32[8,7,8,128]{3,2,1,0:T(8,128)} %get-tuple-element.62), channel_id=1, source_target_pairs={{0,32},{32,64},{64,96},{96,128},{128,160},{160,192},{192,224},{224... | collective-permute-start | bytes 688136 | tf_op jit(solution)/shard_map/ppermute | solution.py:25
  14.6 26.5 %collective-permute-start.3 = (f32[8,16,7,128]{3,2,1,0:T(8,128)}, f32[8,16,7,128]{3,2,1,0:T(8,128)}, u32[]{:S(2)}, u32[]{:S(2)}) collective-permute-start(f32[8,16,7,128]{3,2,1,0:T(8,128)} %get-tuple-element.61), channel_id=1, source_target_pairs={{1,0},{2,1},{3,2},{4,3},{5,4},{6,5},{7,6},{8,7},{9,8},{10,9},{11,1... | collective-permute-start | bytes 1376264 | tf_op jit(solution)/shard_map/ppermute | solution.py:26
  30.3 3.4 %copy-start.40 = (s32[16,8,128]{2,1,0:T(8,128)S(1)}, s32[16,8,128]{2,1,0:T(8,128)}, u32[]{:S(2)}) copy-start(s32[16,8,128]{2,1,0:T(8,128)} %param.7) | copy-start | bytes 196612
  30.3 4.3 %copy-start.41 = (f32[8]{0:T(128)S(1)}, f32[8]{0:T(128)}, u32[]{:S(2)}) copy-start(f32[8]{0:T(128)} %param.9) | copy-start | bytes 100
  40.7 2.1 %copy-start.2 = (f32[1,16,8,128]{3,0,2,1:T(1,128)S(1)}, f32[1,16,8,128]{3,0,2,1:T(1,128)}, u32[]{:S(2)}) copy-start(f32[1,16,8,128]{3,0,2,1:T(1,128)} %get-tuple-element.25) | copy-start | bytes 196612
  40.7 2.1 %copy-start.3 = (f32[1,16,8,128]{3,0,2,1:T(1,128)S(1)}, f32[1,16,8,128]{3,0,2,1:T(1,128)}, u32[]{:S(2)}) copy-start(f32[1,16,8,128]{3,0,2,1:T(1,128)} %get-tuple-element.26) | copy-start | bytes 196612
  40.7 2.1 %copy-start.4 = (f32[1,16,8,128]{3,0,2,1:T(1,128)S(1)}, f32[1,16,8,128]{3,0,2,1:T(1,128)}, u32[]{:S(2)}) copy-start(f32[1,16,8,128]{3,0,2,1:T(1,128)} %get-tuple-element.27) | copy-start | bytes 196612
  40.7 2.1 %copy-start.5 = (f32[1,16,8,128]{3,0,2,1:T(1,128)S(1)}, f32[1,16,8,128]{3,0,2,1:T(1,128)}, u32[]{:S(2)}) copy-start(f32[1,16,8,128]{3,0,2,1:T(1,128)} %get-tuple-element.28) | copy-start | bytes 196612
  40.7 2.1 %copy-start.6 = (f32[1,16,8,128]{3,0,2,1:T(1,128)S(1)}, f32[1,16,8,128]{3,0,2,1:T(1,128)}, u32[]{:S(2)}) copy-start(f32[1,16,8,128]{3,0,2,1:T(1,128)} %get-tuple-element.29) | copy-start | bytes 196612
  40.7 2.1 %copy-start.7 = (f32[1,16,8,128]{3,0,2,1:T(1,128)S(1)}, f32[1,16,8,128]{3,0,2,1:T(1,128)}, u32[]{:S(2)}) copy-start(f32[1,16,8,128]{3,0,2,1:T(1,128)} %get-tuple-element.30) | copy-start | bytes 196612
  40.8 2.1 %copy-start.8 = (f32[1,16,8,128]{3,0,2,1:T(1,128)S(1)}, f32[1,16,8,128]{3,0,2,1:T(1,128)}, u32[]{:S(2)}) copy-start(f32[1,16,8,128]{3,0,2,1:T(1,128)} %get-tuple-element.31) | copy-start | bytes 196612
  40.8 2.1 %copy-start.9 = (f32[1,16,8,128]{3,0,2,1:T(1,128)S(1)}, f32[1,16,8,128]{3,0,2,1:T(1,128)}, u32[]{:S(2)}) copy-start(f32[1,16,8,128]{3,0,2,1:T(1,128)} %get-tuple-element.32) | copy-start | bytes 196612
  40.8 2.1 %copy-start.10 = (f32[1,16,8,128]{3,0,2,1:T(1,128)S(1)}, f32[1,16,8,128]{3,0,2,1:T(1,128)}, u32[]{:S(2)}) copy-start(f32[1,16,8,128]{3,0,2,1:T(1,128)} %get-tuple-element.33) | copy-start | bytes 196612
  40.8 2.1 %copy-start.11 = (f32[1,16,8,128]{3,0,2,1:T(1,128)S(1)}, f32[1,16,8,128]{3,0,2,1:T(1,128)}, u32[]{:S(2)}) copy-start(f32[1,16,8,128]{3,0,2,1:T(1,128)} %get-tuple-element.34) | copy-start | bytes 196612
  40.8 2.1 %copy-start.12 = (f32[1,16,8,128]{3,0,2,1:T(1,128)S(1)}, f32[1,16,8,128]{3,0,2,1:T(1,128)}, u32[]{:S(2)}) copy-start(f32[1,16,8,128]{3,0,2,1:T(1,128)} %get-tuple-element.35) | copy-start | bytes 196612
  40.8 2.1 %copy-start.13 = (f32[1,16,8,128]{3,0,2,1:T(1,128)S(1)}, f32[1,16,8,128]{3,0,2,1:T(1,128)}, u32[]{:S(2)}) copy-start(f32[1,16,8,128]{3,0,2,1:T(1,128)} %get-tuple-element.36) | copy-start | bytes 196612
  40.8 2.1 %copy-start.14 = (f32[1,16,8,128]{3,0,2,1:T(1,128)S(1)}, f32[1,16,8,128]{3,0,2,1:T(1,128)}, u32[]{:S(2)}) copy-start(f32[1,16,8,128]{3,0,2,1:T(1,128)} %get-tuple-element.37) | copy-start | bytes 196612
  48.7 4.2 %copy-start.39 = (f32[32,32]{1,0:T(8,128)S(1)}, f32[32,32]{1,0:T(8,128)}, u32[]{:S(2)}) copy-start(f32[32,32]{1,0:T(8,128)} %fusion.6) | copy-start | bytes 12292
  162.4 6.3 %copy-start.38 = (f32[32,8]{0,1:T(8,128)}, f32[32,8]{0,1:T(8,128)S(1)}, u32[]{:S(2)}) copy-start(f32[32,8]{0,1:T(8,128)S(1)} %broadcast_multiply_fusion) | copy-start | bytes 3076
  (22 other events, 46.8 us)
where the time goes:
time: 171 us; the launch traced here: 170 us
  blocking collectives  109 us (64%)
  starting transfers between devices  23.2 us (14%)
  matrix products  15.3 us (9%)
  other arithmetic  11.5 us (7%)
  local copies, waits for them, and re-layouts  9.46 us (6%)
    psum x4, blocking collectives, one_axis_at_a_time(): value = lax.psum(value, axis)  109 us
    ppermute x2, starting transfers between devices, extended(): lax.ppermute(initial, axis, [(b, a) for a, b in up])  13.8 us
    ppermute x2, starting transfers between devices, extended(): lax.ppermute(last, axis, up)  9.37 us
    sub x1, other arithmetic, apply_taps(): image = image - coefs[2 * REACH * dim + j][None] * shifted  5.47 us
    slice x3, local copies, waits for them, and re-layouts, apply_taps(): image = image - coefs[2 * REACH * dim + j][None] * shifted  4.4 us
    dot_general x1, matrix products, per_device(): local_qq = jnp.dot(basis_flat, basis_flat.T, precision=highest)  3.45 us
  transfers between devices with their start and end apart: 4, of which 0 were waited for; matrix products, arithmetic and copies ran while one was open for 8% of the time, Pallas kernels for 0%

commit v1 on v0

v1 whole, which is shorter than its diff:
```python
import functools

import jax
import jax.numpy as jnp
from jax import lax
from jax.experimental import pallas as pl
from jax.experimental.pallas import tpu as pltpu
from jax.sharding import Mesh
from jax.sharding import PartitionSpec as P

COLS = 8
BLOCKS = 4
REACH = 7
MAT = 8
PORTS = 8
AXES = ("gx_0", "gx_1", "gy_0", "gy_1")
GX = ("gx_0", "gx_1")
GY = ("gy_0", "gy_1")
SUB = 8
LANES = 128
HIGHEST = lax.Precision.HIGHEST
F32 = jnp.float32
BF16 = jnp.bfloat16
VMEM = pl.BlockSpec(memory_space=pltpu.VMEM)
HBM = pl.BlockSpec(memory_space=pltpu.MemorySpace.HBM)

QQ_AT = (0, 8, 24, 48)
QW_AT = 80
WW_AT = 112


def in_hbm(value):
    return pltpu.with_memory_space_constraint(value, pltpu.MemorySpace.HBM)


def limit(mebibytes):
    return pltpu.CompilerParams(vmem_limit_bytes=mebibytes * 2**20)


def offset_of(j):
    return j - REACH if j < REACH else j - REACH + 1


def index_of(k):
    return k + REACH if k < 0 else k + REACH - 1


def iota(shape, dim):
    return lax.broadcasted_iota(jnp.int32, shape, dim)


def split(value):
    high = value.astype(BF16)
    return high, (value - high.astype(F32)).astype(BF16)


def rows_dot(a, b, precision=None):
    return lax.dot_general(
        a, b, (((1,), (1,)), ((), ())), precision=precision, preferred_element_type=F32
    )


def plain_dot(a, b, precision=None):
    return lax.dot_general(
        a, b, (((1,), (0,)), ((), ())), precision=precision, preferred_element_type=F32
    )


def shift_of(totals):
    return jnp.mean(totals, axis=0, keepdims=True)


def wide_lanes(value, room):
    room[...] = jnp.zeros(room.shape, F32)
    room[:, : value.shape[1]] = value
    return room[...]


def odd_place(axes):
    place = 0
    for axis in axes:
        place = place * lax.axis_size(axis) + lax.axis_index(axis)
    return lax.rem(place, 2)


def edges_kernel(basis_ref, block_ref, xa_ref, xb_ref, sems):
    odd = odd_place(GX)
    block = basis_ref.at[(BLOCKS - 1) * COLS : BLOCKS * COLS]
    far = basis_ref.shape[1] - REACH
    jobs = (
        (block, block_ref),
        (block.at[:, pl.ds((1 - odd) * far, REACH)], xa_ref),
        (block.at[:, pl.ds(odd * far, REACH)], xb_ref),
    )
    copies = [pltpu.make_async_copy(*job, sems.at[i]) for i, job in enumerate(jobs)]
    for copy in copies:
        copy.start()
    for copy in copies:
        copy.wait()


def local_kernel(taps_ref, gain_ref, basis_ref, block_ref, classes_hbm, ports_hbm,
                 part_ref, coef_x_ref, coef_y_ref, both_ref, sums_ref,
                 along_x, along_y, gains, room, spread, coefs, whole, classes_ref, ports_ref, sems):
    size_x = classes_ref.shape[0]
    jobs = ((classes_hbm, classes_ref), (ports_hbm, ports_ref), (basis_ref, whole))
    *loads, load = [pltpu.make_async_copy(*job, sems.at[i]) for i, job in enumerate(jobs)]
    for copy in (*loads, load):
        copy.start()
    row = iota((SUB, LANES), 0)
    lane = iota((SUB, LANES), 1)
    taps = wide_lanes(taps_ref[...], room)
    totals = jnp.broadcast_to(jnp.sum(taps, axis=1, keepdims=True), (MAT, LANES))
    taps = jnp.where(lane == 6 * REACH, totals - shift_of(totals), taps)
    high, rest = split(taps)
    middle, low = split((taps - high.astype(F32)))
    each = jnp.concatenate([high.astype(F32), middle.astype(F32), low.astype(F32)], axis=0)
    each = jnp.broadcast_to(each[:, None, :], (3 * MAT, SUB, LANES)).reshape(3 * MAT * SUB, LANES)
    count = 6 * REACH + 1
    chosen = (iota((count * SUB, LANES), 0) // SUB == iota((count * SUB, LANES), 1)).astype(BF16)
    by_kind = rows_dot(chosen, each.astype(BF16))
    same = (iota(by_kind.shape, 0) % SUB) == (iota(by_kind.shape, 1) % SUB)
    spread[...] = jnp.where(same, by_kind, 0.0).astype(BF16)
    gain = wide_lanes(jnp.broadcast_to(gain_ref[...], (SUB, PORTS)), room)
    for p in range(PORTS):
        gains[p] = jnp.broadcast_to(gain[:, p : p + 1], (SUB, LANES))
    zero = jnp.zeros((SUB, LANES), F32)
    for x in range(REACH):
        for c in range(COLS):
            along_x[x, c] = zero
            along_x[REACH + size_x + x, c] = zero

    def prepare(x, carry):
        for c in range(COLS):
            v = block_ref[c, x]
            along_x[REACH + x, c] = v
            along_y[x, c, 0:SUB] = v
            along_y[x, c, SUB : 2 * SUB] = v
        return carry

    lax.fori_loop(0, size_x, prepare, 0)
    for copy in loads:
        copy.wait()

    def hot(x):
        kind = classes_ref[x]
        one = jnp.concatenate([(kind == m).astype(F32) for m in range(MAT)], axis=0).astype(BF16)
        return jnp.concatenate([one, one, one], axis=0)

    def plane(x, at):
        port = ports_ref[x]
        coef_at = lambda t: coefs[t * SUB : (t + 1) * SUB, at * LANES : (at + 1) * LANES]
        own = [along_x[REACH + x, c] for c in range(COLS)]
        diag = coef_at(6 * REACH)
        extra = zero
        for p in range(PORTS):
            extra = jnp.where(port == p + 1, gains[p], extra)
        diag = diag + extra
        acc = [diag * v for v in own]
        for j in range(2 * REACH):
            coef = coef_at(j)
            for c in range(COLS):
                acc[c] = acc[c] - coef * along_x[REACH + x + offset_of(j), c]
        for j in range(REACH):
            coef_x_ref[x, j] = jnp.where(x < size_x // 2, coef_at(j), coef_at(REACH + j))
        for k in range(1, REACH + 1):
            up = coef_at(2 * REACH + index_of(k))
            down = coef_at(2 * REACH + index_of(k - SUB))
            inside = row < SUB - k
            coef = jnp.where(inside, up, down)
            coef_y_ref[x, k - 1] = jnp.where(inside, down, up)
            for c in range(COLS):
                acc[c] = acc[c] - coef * along_y[x, c, k : k + SUB]
        for j in range(2 * REACH):
            k = offset_of(j)
            coef = jnp.where((lane + k >= 0) & (lane + k < LANES), coef_at(4 * REACH + j), 0.0)
            for c in range(COLS):
                acc[c] = acc[c] - coef * pltpu.roll(own[c], (-k) % LANES, 1)
        for c in range(COLS):
            part_ref[x, c] = acc[c]

    def pair(i, carry):
        coefs[...] = plain_dot(spread[...], jnp.concatenate([hot(2 * i), hot(2 * i + 1)], axis=1))
        plane(2 * i, 0)
        plane(2 * i + 1, 1)
        return carry

    lax.fori_loop(0, size_x // 2, pair, 0)

    load.wait()
    wide = BLOCKS * COLS
    lines = size_x * SUB

    def store(x, carry):
        for y in range(SUB):
            high, low = split(whole[pl.ds(x * SUB + y, wide, stride=lines), :])
            at = pl.ds(pl.multiple_of((x * SUB + y) * LANES, LANES), LANES)
            both_ref[:, at] = jnp.concatenate([high, low], axis=0)
        return carry

    lax.fori_loop(0, size_x, store, 0)
    both = both_ref[...]
    products = rows_dot(both, both)
    products = jnp.concatenate([products, jnp.zeros((2 * wide, LANES - 2 * wide), F32)], axis=1)
    products = products[:wide] + products[wide:]
    products = products + pltpu.roll(products, LANES - wide, 1)
    sums = zero
    for a in range(BLOCKS):
        block = jnp.where(lane < (a + 1) * COLS, products[a * COLS : (a + 1) * COLS], 0.0)
        sums = sums + (pltpu.roll(block, QQ_AT[a], 1) if QQ_AT[a] else block)
    sums_ref[...] = sums


def halo_kernel(part_ref, coef_x_ref, coef_y_ref, both_ref, sums_ref,
                xa_ref, xb_ref, ya_ref, yb_ref,
                w_ref, out_ref, around, image, room):
    size_x = part_ref.shape[0]
    odd_x = odd_place(GX) == 1
    odd_y = odd_place(GY)
    below_x = lambda p, c: jnp.where(odd_x, xa_ref[c, p], xb_ref[c, p])
    above_x = lambda p, c: jnp.where(odd_x, xb_ref[c, p], xa_ref[c, p])
    at_a = pl.ds(pl.multiple_of((1 - odd_y) * SUB, SUB), SUB)
    at_b = pl.ds(pl.multiple_of(odd_y * SUB, SUB), SUB)
    lines = size_x * SUB
    for x in range(size_x):
        for c in range(COLS):
            around[x, c, at_a] = ya_ref[c, x]
            around[x, c, at_b] = yb_ref[c, x]
        acc = [part_ref[x, c] for c in range(COLS)]
        for k in range(1, REACH + 1):
            coef = coef_y_ref[x, k - 1]
            for c in range(COLS):
                acc[c] = acc[c] - coef * around[x, c, k : k + SUB]
        for j in range(2 * REACH):
            at = x + offset_of(j)
            if 0 <= at < size_x:
                continue
            coef = coef_x_ref[x, j % REACH]
            for c in range(COLS):
                value = below_x(at + REACH, c) if at < 0 else above_x(at - size_x, c)
                acc[c] = acc[c] - coef * value
        for c in range(COLS):
            image[c * lines + x * SUB : c * lines + (x + 1) * SUB, :] = acc[c]
        for y in range(SUB):
            high, low = split(image[pl.ds(x * SUB + y, COLS, stride=lines), :])
            at = (x * SUB + y) * LANES
            w_ref[:, at : at + LANES] = jnp.concatenate([high, low], axis=0)
    w = w_ref[...]
    wide = BLOCKS * COLS
    lane = iota((SUB, LANES), 1)
    q_w = wide_lanes(rows_dot(w, both_ref[...]), room)
    q_w = q_w[:COLS] + q_w[COLS:]
    q_w = jnp.where(lane < wide, q_w + pltpu.roll(q_w, LANES - wide, 1), 0.0)
    w_w = wide_lanes(rows_dot(w, w), room)
    w_w = w_w[:COLS] + w_w[COLS:]
    w_w = jnp.where(lane < COLS, w_w + pltpu.roll(w_w, LANES - COLS, 1), 0.0)
    out_ref[...] = sums_ref[...] + pltpu.roll(q_w, QW_AT, 1) + pltpu.roll(w_w, WW_AT, 1)


def fold_kernel(*refs):
    *tiles, out_ref = refs
    total = sum(jnp.sum(tile[...], axis=0) if tile.ndim == 3 else tile[...] for tile in tiles)
    out_ref[...] = jnp.broadcast_to(total[None], out_ref.shape)


def root_inverse(value):
    guess = lax.rsqrt(value)
    return guess * (1.5 - 0.5 * value * guess * guess)


def finish_kernel(scale, taps_ref, received_ref, both_ref, w_ref,
                  next_ref, projection_ref, triangle_ref, room, result, sems):
    size_x = next_ref.shape[1] // SUB
    wide = BLOCKS * COLS
    row = iota((SUB, LANES), 0)
    lane = iota((SUB, LANES), 1)
    sums = jnp.sum(received_ref[...], axis=0) * scale
    taps = wide_lanes(taps_ref[...], room)
    totals = jnp.broadcast_to(jnp.sum(taps, axis=1, keepdims=True), (MAT, LANES))
    shift = 1.0 + shift_of(totals)
    part_t = jnp.where(lane < wide, pltpu.roll(sums, LANES - QW_AT, 1), 0.0)
    w_w = jnp.where(lane < COLS, pltpu.roll(sums, LANES - WW_AT, 1), 0.0)
    blocks = []
    for a in range(BLOCKS):
        block = pltpu.roll(sums, LANES - QQ_AT[a], 1) if QQ_AT[a] else sums
        block = jnp.where(lane < (a + 1) * COLS, block, 0.0)
        last = block
        blocks.append(jnp.where(lane >= a * COLS, 0.5 * block, block))
    unit = jnp.where(lane == row + (wide - COLS), 1.0, 0.0)
    p_t = part_t + shift * last
    back_t = shift * (unit - last) - part_t
    lower = jnp.concatenate(blocks + [jnp.zeros((LANES - wide, LANES), F32)], axis=0)
    rest = jnp.zeros((LANES - SUB, LANES), F32)
    inner = part_t + plain_dot(back_t, lower, HIGHEST)
    gram = (
        w_w
        + rows_dot(inner, jnp.concatenate([back_t, rest], axis=0), HIGHEST)
        + rows_dot(back_t, jnp.concatenate([inner, rest], axis=0), HIGHEST)
    )
    apply = jnp.where(lane == row + wide, 1.0, back_t)
    for k in range(COLS):
        column = jnp.broadcast_to(gram[:, k : k + 1], (SUB, LANES))
        pivot = jnp.broadcast_to(gram[k : k + 1, k : k + 1], (SUB, LANES))
        inverse = root_inverse(pivot)
        gram_row = jnp.broadcast_to(gram[k : k + 1, :], (SUB, LANES)) * inverse
        apply_row = jnp.broadcast_to(apply[k : k + 1, :], (SUB, LANES)) * inverse
        factor = jnp.where(row > k, column * inverse, 0.0)
        gram = jnp.where(row == k, gram_row, gram - factor * gram_row)
        apply = jnp.where(row == k, apply_row, apply - factor * apply_row)
    triangle_ref[...] = jnp.where(lane >= row, gram, 0.0)[:, :COLS]
    projection_ref[...] = p_t[:, :wide]
    high, low = split(apply)
    pieces = jnp.concatenate([high.astype(F32), low.astype(F32)], axis=0)
    lane = iota(pieces.shape, 1)
    on_both = jnp.where(lane < wide, pieces, pltpu.roll(pieces, wide, 1))[:, : 2 * wide].astype(BF16)
    pieces = pltpu.roll(pieces, LANES - wide, 1)
    on_w = jnp.where(lane < COLS, pieces, pltpu.roll(pieces, COLS, 1))[:, : 2 * COLS].astype(BF16)
    lines = size_x * SUB
    group = size_x // 4
    copies = []
    for x in range(size_x):
        at = slice(x * SUB * LANES, (x + 1) * SUB * LANES)
        block = plain_dot(on_both, both_ref[:, at]) + plain_dot(on_w, w_ref[:, at])
        block = block[:COLS] + block[COLS:]
        for y in range(SUB):
            result[pl.ds(x * SUB + y, COLS, stride=lines), :] = block[:, y * LANES : (y + 1) * LANES]
        if x % group == group - 1:
            for c in range(COLS):
                copies.append(pltpu.make_async_copy(
                    result.at[pl.ds(c * lines + (x + 1 - group) * SUB, group * SUB)],
                    next_ref.at[c, pl.ds((x + 1 - group) * SUB, group * SUB)],
                    sems.at[x // group, c],
                ))
                copies[-1].start()
    for copy in copies:
        copy.wait()


def swaps(devices):
    first = [(i, i ^ 1) for i in range(devices)]
    second = [pair for i in range(1, devices - 1, 2) for pair in ((i, i + 1), (i + 1, i))]
    return first, second


def per_device(basis, classes, ports, taps, port_gain):
    size_x, size_y, size_z = classes.shape
    x_first, x_second = swaps(lax.axis_size(GX))
    y_first, y_second = swaps(lax.axis_size(GY))
    shape = jax.ShapeDtypeStruct
    wide, cells, lines = BLOCKS * COLS, size_x * size_y * size_z, size_x * SUB
    tile = shape((SUB, LANES), F32)
    edge = shape((COLS, REACH, SUB, LANES), F32)
    block, xa, xb = pl.pallas_call(
        edges_kernel,
        out_shape=(shape((COLS, size_x, SUB, LANES), F32), edge, edge),
        in_specs=[HBM],
        out_specs=(VMEM,) * 3,
        scratch_shapes=[pltpu.SemaphoreType.DMA((3,))],
        compiler_params=limit(4),
        name="edges",
    )(in_hbm(basis))
    yb = lax.ppermute(block, GY, y_second)
    xb = lax.ppermute(xb, GX, x_second)
    xa = lax.ppermute(xa, GX, x_first)
    ya = lax.ppermute(block, GY, y_first)
    part, coef_x, coef_y, both, sums = pl.pallas_call(
        local_kernel,
        out_shape=(
            shape((size_x, COLS, SUB, LANES), F32),
            shape((size_x, REACH, SUB, LANES), F32),
            shape((size_x, REACH, SUB, LANES), F32),
            shape((2 * wide, cells), BF16),
            tile,
        ),
        in_specs=[VMEM, VMEM, HBM, VMEM, HBM, HBM],
        out_specs=(VMEM,) * 5,
        scratch_shapes=[
            pltpu.VMEM((size_x + 2 * REACH, COLS, SUB, LANES), F32),
            pltpu.VMEM((size_x, COLS, 2 * SUB, LANES), F32),
            pltpu.VMEM((PORTS, SUB, LANES), F32),
            pltpu.VMEM((SUB, LANES), F32),
            pltpu.VMEM(((6 * REACH + 1) * SUB, 3 * MAT * SUB), BF16),
            pltpu.VMEM(((6 * REACH + 1) * SUB, 2 * LANES), F32),
            pltpu.VMEM((wide * lines, LANES), F32),
            pltpu.VMEM((size_x, SUB, LANES), jnp.int32),
            pltpu.VMEM((size_x, SUB, LANES), jnp.int32),
            pltpu.SemaphoreType.DMA((3,)),
        ],
        compiler_params=limit(16),
        cost_estimate=pl.CostEstimate(flops=10**9, bytes_accessed=8 * 2**20, transcendentals=0),
        name="local",
    )(taps, port_gain[None], in_hbm(basis.reshape(wide * lines, LANES)), block, in_hbm(classes), in_hbm(ports))
    w, sums = pl.pallas_call(
        halo_kernel,
        out_shape=(shape((2 * COLS, cells), BF16), tile),
        in_specs=[VMEM] * 9,
        out_specs=(VMEM,) * 2,
        scratch_shapes=[
            pltpu.VMEM((size_x, COLS, 2 * SUB, LANES), F32),
            pltpu.VMEM((COLS * lines, LANES), F32),
            pltpu.VMEM((2 * COLS, LANES), F32),
        ],
        compiler_params=limit(8),
        name="halo",
    )(part, coef_x, coef_y, both, sums, xa, xb, ya, yb)

    def fold(copies, *tiles):
        return pl.pallas_call(
            fold_kernel,
            out_shape=shape((copies, SUB, LANES), F32),
            in_specs=[VMEM] * len(tiles),
            out_specs=VMEM,
            compiler_params=limit(2),
            name="fold",
        )(*tiles)

    beside = lax.ppermute(sums, "gy_1", [(0, 1), (1, 0)])
    along_gx = lax.all_to_all(fold(lax.axis_size(GX), sums, beside), GX, 0, 0)
    received = lax.all_to_all(fold(lax.axis_size("gy_0"), along_gx), "gy_0", 0, 0)
    total = cells * lax.axis_size(GX) * lax.axis_size(GY)
    next_block, projection, triangle = pl.pallas_call(
        functools.partial(finish_kernel, 1.0 / total),
        out_shape=(
            shape((COLS, lines, LANES), F32),
            shape((COLS, wide), F32),
            shape((COLS, COLS), F32),
        ),
        in_specs=[VMEM] * 4,
        out_specs=(HBM, VMEM, VMEM),
        scratch_shapes=[
            pltpu.VMEM((MAT, LANES), F32),
            pltpu.VMEM((COLS * lines, LANES), F32),
            pltpu.SemaphoreType.DMA((4, COLS)),
        ],
        compiler_params=limit(8),
        name="finish",
    )(taps, received, both, w)
    return next_block.reshape(COLS, size_x, size_y, size_z), projection.T, triangle


def solution(mesh):
    split_mesh = Mesh(mesh.devices.reshape(4, 8, 16, 2), AXES)
    in_specs = (P(None, GX, GY, None), P(GX, GY, None), P(GX, GY, None), P(), P())
    out_specs = (P(None, GX, GY, None), P(), P())
    return jax.shard_map(
        per_device, mesh=split_mesh, in_specs=in_specs, out_specs=out_specs, check_vma=False
    )
```

time: 171 us -> 80.4 us (0.47)
  the two profiles are of different devices: /device:TPU:1 before, /device:TPU:8 now
where the time goes in v1:
time: 80.4 us; the launch traced here: 80.1 us
  blocking collectives  42.6 us (53%)
  starting transfers between devices  21.5 us (27%)
  Pallas kernels  13 us (16%)
  waiting for transfers between devices  2.3 us (3%)
    all_to_all x1, blocking collectives, per_device(): lax.all_to_all(fold(lax.axis_size('gy_0'), along_gx), 'gy_0', 0, 0)  29 us
    all_to_all x1, blocking collectives, per_device(): along_gx = lax.all_to_all(fold(lax.axis_size(GX), sums, beside), GX, 0, 0)  13.6 us
    ppermute x1, starting transfers between devices, per_device(): xa = lax.ppermute(xa, GX, x_first)  11.3 us
    pallas_call x1, Pallas kernels, per_device(): pl.pallas_call(local_kernel, out_shape=(shape((size_x, COLS, SUB, LANES),...  6.49 us
    ppermute x1, starting transfers between devices, per_device(): ya = lax.ppermute(block, GY, y_first)  5.61 us
    pallas_call x1, Pallas kernels, per_device(): pl.pallas_call(functools.partial(finish_kernel, 1.0 / total), out_shape=(...  3.51 us
    ppermute x1, starting transfers between devices, per_device(): beside = lax.ppermute(sums, 'gy_1', [(0, 1), (1, 0)])  1.94 us
    ppermute x1, starting transfers between devices, per_device(): xb = lax.ppermute(xb, GX, x_second)  1.92 us
  transfers between devices with their start and end apart: 5, of which 2 were waited for; matrix products, arithmetic and copies ran while one was open for 0% of the time, Pallas kernels for 8%

profile of v1, /device:TPU:8, one launch (start us, length us, event | category | flops | bytes accessed | tf_op | source)
XLA Modules:
  0.0 80.1 jit_solution(16021493928792427385)
XLA Ops:
  0.6 0.0 copy-start
  0.6 0.0 copy-start.1
  0.7 1.2 %edges.1 = (f32[8,16,8,128]{3,2,1,0:T(8,128)S(1)}, f32[8,7,8,128]{3,2,1,0:T(8,128)S(1)}, f32[8,7,8,128]{3,2,1,0:T(8,128)S(1)}) custom-call(f32[32,16,8,128]{3,2,1,0:T(8,128)} %basis_ref.1), custom_call_target="tpu_custom_call" | custom-call | tf_op jit(solution)/shard_map/edges/pallas_call | solution.py:353
  1.9 0.7 collective-permute-start.3
  2.6 5.6 %collective-permute-start.2 = (f32[8,16,8,128]{3,2,1,0:T(8,128)S(1)}, f32[8,16,8,128]{3,2,1,0:T(8,128)S(1)}, u32[]{:S(2)}, u32[]{:S(2)}) collective-permute-start(f32[8,16,8,128]{3,2,1,0:T(8,128)S(1)} %get-tuple-element.16.block_ref), channel_id=1, source_target_pairs={{0,1},{1,0},{2,3},{3,2},{4,5},{5,4},{6,7},{7,6},{8,9},{9,8},{10,11... | collective-permute-start | bytes 1572872 | tf_op jit(solution)/shard_map/ppermute | solution.py:365
  8.2 11.3 %collective-permute-start = (f32[8,7,8,128]{3,2,1,0:T(8,128)S(1)}, f32[8,7,8,128]{3,2,1,0:T(8,128)S(1)}, u32[]{:S(2)}, u32[]{:S(2)}) collective-permute-start(f32[8,7,8,128]{3,2,1,0:T(8,128)S(1)} %get-tuple-element.22), channel_id=1, source_target_pairs={{0,32},{32,0},{64,96},{96,64},{128,160},{160,128},{192,224},{224,1... | collective-permute-start | bytes 688136 | tf_op jit(solution)/shard_map/ppermute | solution.py:364
  19.5 1.9 %collective-permute-start.1 = (f32[8,7,8,128]{3,2,1,0:T(8,128)S(1)}, f32[8,7,8,128]{3,2,1,0:T(8,128)S(1)}, u32[]{:S(2)}, u32[]{:S(2)}) collective-permute-start(f32[8,7,8,128]{3,2,1,0:T(8,128)S(1)} %get-tuple-element.23), channel_id=1, source_target_pairs={{32,64},{64,32},{96,128},{128,96},{160,192},{192,160},{224,256},{2... | collective-permute-start | bytes 688136 | tf_op jit(solution)/shard_map/ppermute | solution.py:363
  21.4 0.0 copy-done
  21.4 0.0 copy-done.1
  21.4 6.5 %local.1 = (f32[16,8,8,128]{3,2,1,0:T(8,128)S(1)}, f32[16,7,8,128]{3,2,1,0:T(8,128)S(1)}, f32[16,7,8,128]{3,2,1,0:T(8,128)S(1)}, bf16[64,16384]{1,0:T(8,128)(2,1)S(1)}, f32[8,128]{1,0:T(8,128)S(1)}) custom-call(f32[8,42]{1,0:T(8,128)S(1)} %copy-done, f32[1,8]{1,0:T(1,128)S(1)} %bitcast.4, f32[4096,128]{1,0:T(8,128)} %bitcast.5, ...), custom_call_target="tpu_custom_call" | custom-call | flops 1000000000 | bytes 8388608 | tf_op jit(solution)/shard_map/local/pallas_call | solution.py:366
  27.9 0.0 collective-permute-done.xa_ref
  27.9 1.2 %collective-permute-done.1.xb_ref = f32[8,7,8,128]{3,2,1,0:T(8,128)S(1)} collective-permute-done((f32[8,7,8,128]{3,2,1,0:T(8,128)S(1)}, f32[8,7,8,128]{3,2,1,0:T(8,128)S(1)}, u32[]{:S(2)}, u32[]{:S(2)}) %collective-permute-start.1) | collective-permute-done | bytes 229408 | tf_op jit(solution)/shard_map/ppermute | solution.py:363
  29.1 0.0 collective-permute-done.3.yb_ref
  29.1 0.0 collective-permute-done.2.ya_ref
  29.1 1.8 %halo.1 = (bf16[16,16384]{1,0:T(8,128)(2,1)S(1)}, f32[8,128]{1,0:T(8,128)S(1)}) custom-call(f32[16,8,8,128]{3,2,1,0:T(8,128)S(1)} %get-tuple-element.17.part_ref, f32[16,7,8,128]{3,2,1,0:T(8,128)S(1)} %get-tuple-element.18.coef_x_ref, f32[16,7,8,128]{3,2,1,0:T(8,128)S(1)} %get-tuple-element.19.coef_y_ref, bf16[64,16384]{1,0:T(8,128)(2,1)S(1)} %get-tuple-element.20.both_ref, ...), custom_call_target="tpu_custom_call" | custom-call | tf_op jit(solution)/shard_map/halo/pallas_call | solution.py:393
  30.9 1.9 %collective-permute-start.4 = (f32[8,128]{1,0:T(8,128)S(1)}, f32[8,128]{1,0:T(8,128)S(1)}, u32[]{:S(2)}, u32[]{:S(2)}) collective-permute-start(f32[8,128]{1,0:T(8,128)S(1)} %get-tuple-element.24.refs_0_), channel_id=1, source_target_pairs={{0,1},{1,0},{2,3},{3,2},{4,5},{5,4},{6,7},{7,6},{8,9},{9,8},{10,11... | collective-permute-start | bytes 12296 | tf_op jit(solution)/shard_map/ppermute | solution.py:417
  32.8 1.1 %collective-permute-done.4.refs_1_ = f32[8,128]{1,0:T(8,128)S(1)} collective-permute-done((f32[8,128]{1,0:T(8,128)S(1)}, f32[8,128]{1,0:T(8,128)S(1)}, u32[]{:S(2)}, u32[]{:S(2)}) %collective-permute-start.4) | collective-permute-done | bytes 4128 | tf_op jit(solution)/shard_map/ppermute | solution.py:417
  34.0 13.6 %all_to_all.10.refs_0_ = f32[32,8,128]{2,1,0:T(8,128)S(1)} all-to-all(f32[32,8,128]{2,1,0:T(8,128)S(1)} %fold.2), channel_id=1, replica_groups=mesh['gx_0'=4,'gx_1'=8,'gy_0'=16,'gy_1'=2] {'gx_0','gx_1'}, dimensions={0} | all-to-all | bytes 262144 | tf_op jit(solution)/shard_map/all_to_all | solution.py:418
  47.6 29.0 %all_to_all.11.received_ref = f32[16,8,128]{2,1,0:T(8,128)S(1)} all-to-all(f32[16,8,128]{2,1,0:T(8,128)S(1)} %fold.3), channel_id=1, replica_groups=mesh['gx_0'=4,'gx_1'=8,'gy_0'=16,'gy_1'=2] {'gy_0'}, dimensions={0} | all-to-all | bytes 131072 | tf_op jit(solution)/shard_map/all_to_all | solution.py:419
  76.6 3.5 %finish.1 = (f32[8,128,128]{2,1,0:T(8,128)}, f32[8,32]{1,0:T(8,128)}, f32[8,8]{1,0:T(8,128)}) custom-call(f32[8,42]{1,0:T(8,128)S(1)} %copy-done, f32[16,8,128]{2,1,0:T(8,128)S(1)} %all_to_all.11.received_ref, bf16[64,16384]{1,0:T(8,128)(2,1)S(1)} %get-tuple-element.20.both_ref, bf16[16,16384]{1,0:T(8,128)(2,1)S(1)} %get-tuple-element.25.w_ref), custom_call_target="tpu_custom_call" | custom-call | tf_op jit(solution)/shard_map/finish/pallas_call | solution.py:421
  (2 shorter events, 0.0 us)
Async XLA Ops:
  0.6 20.8 %copy-start = (f32[8,42]{1,0:T(8,128)S(1)}, f32[8,42]{1,0:T(8,128)}, u32[]{:S(2)}) copy-start(f32[8,42]{1,0:T(8,128)} %taps_ref.3) | copy-start | bytes 4036
  0.6 20.8 %copy-start.1 = (f32[8]{0:T(128)S(1)}, f32[8]{0:T(128)}, u32[]{:S(2)}) copy-start(f32[8]{0:T(128)} %param.9) | copy-start | bytes 100
  1.9 27.2 %collective-permute-start.3 = (f32[8,16,8,128]{3,2,1,0:T(8,128)S(1)}, f32[8,16,8,128]{3,2,1,0:T(8,128)S(1)}, u32[]{:S(2)}, u32[]{:S(2)}) collective-permute-start(f32[8,16,8,128]{3,2,1,0:T(8,128)S(1)} %get-tuple-element.16.block_ref), channel_id=1, source_target_pairs={{1,2},{2,1},{3,4},{4,3},{5,6},{6,5},{7,8},{8,7},{9,10},{10,9},{11,... | collective-permute-start | bytes 1572872 | tf_op jit(solution)/shard_map/ppermute | solution.py:362
  2.6 26.5 %collective-permute-start.2 = (f32[8,16,8,128]{3,2,1,0:T(8,128)S(1)}, f32[8,16,8,128]{3,2,1,0:T(8,128)S(1)}, u32[]{:S(2)}, u32[]{:S(2)}) collective-permute-start(f32[8,16,8,128]{3,2,1,0:T(8,128)S(1)} %get-tuple-element.16.block_ref), channel_id=1, source_target_pairs={{0,1},{1,0},{2,3},{3,2},{4,5},{5,4},{6,7},{7,6},{8,9},{9,8},{10,11... | collective-permute-start | bytes 1572872 | tf_op jit(solution)/shard_map/ppermute | solution.py:365
  8.2 19.7 %collective-permute-start = (f32[8,7,8,128]{3,2,1,0:T(8,128)S(1)}, f32[8,7,8,128]{3,2,1,0:T(8,128)S(1)}, u32[]{:S(2)}, u32[]{:S(2)}) collective-permute-start(f32[8,7,8,128]{3,2,1,0:T(8,128)S(1)} %get-tuple-element.22), channel_id=1, source_target_pairs={{0,32},{32,0},{64,96},{96,64},{128,160},{160,128},{192,224},{224,1... | collective-permute-start | bytes 688136 | tf_op jit(solution)/shard_map/ppermute | solution.py:364
  19.5 9.6 %collective-permute-start.1 = (f32[8,7,8,128]{3,2,1,0:T(8,128)S(1)}, f32[8,7,8,128]{3,2,1,0:T(8,128)S(1)}, u32[]{:S(2)}, u32[]{:S(2)}) collective-permute-start(f32[8,7,8,128]{3,2,1,0:T(8,128)S(1)} %get-tuple-element.23), channel_id=1, source_target_pairs={{32,64},{64,32},{96,128},{128,96},{160,192},{192,160},{224,256},{2... | collective-permute-start | bytes 688136 | tf_op jit(solution)/shard_map/ppermute | solution.py:363
  30.9 3.1 %collective-permute-start.4 = (f32[8,128]{1,0:T(8,128)S(1)}, f32[8,128]{1,0:T(8,128)S(1)}, u32[]{:S(2)}, u32[]{:S(2)}) collective-permute-start(f32[8,128]{1,0:T(8,128)S(1)} %get-tuple-element.24.refs_0_), channel_id=1, source_target_pairs={{0,1},{1,0},{2,3},{3,2},{4,5},{5,4},{6,7},{7,6},{8,9},{9,8},{10,11... | collective-permute-start | bytes 12296 | tf_op jit(solution)/shard_map/ppermute | solution.py:417

commit v2 on v1

--- a/solution.py
+++ b/solution.py
@@ -101,18 +101,21 @@
 
 def local_kernel(taps_ref, gain_ref, basis_ref, block_ref, classes_hbm, ports_hbm,
                  part_ref, coef_x_ref, coef_y_ref, both_ref, sums_ref,
-                 along_x, along_y, gains, room, spread, coefs, whole, classes_ref, ports_ref, sems):
+                 along_x, along_y, gains, room, spread, hots, coefs, whole, own, shifts, shifted,
+                 classes_ref, ports_ref, sems):
     size_x = classes_ref.shape[0]
-    jobs = ((classes_hbm, classes_ref), (ports_hbm, ports_ref), (basis_ref, whole))
-    *loads, load = [pltpu.make_async_copy(*job, sems.at[i]) for i, job in enumerate(jobs)]
-    for copy in (*loads, load):
+    wide = BLOCKS * COLS
+    jobs = ((classes_hbm, classes_ref), (ports_hbm, ports_ref))
+    loads = [pltpu.make_async_copy(*job, sems.at[i]) for i, job in enumerate(jobs)]
+    basis_loads = [pltpu.make_async_copy(basis_ref.at[c], whole.at[:, c], sems.at[2 + c]) for c in range(wide)]
+    for copy in (*loads, *basis_loads):
         copy.start()
     row = iota((SUB, LANES), 0)
     lane = iota((SUB, LANES), 1)
     taps = wide_lanes(taps_ref[...], room)
     totals = jnp.broadcast_to(jnp.sum(taps, axis=1, keepdims=True), (MAT, LANES))
     taps = jnp.where(lane == 6 * REACH, totals - shift_of(totals), taps)
-    high, rest = split(taps)
+    high, _ = split(taps)
     middle, low = split((taps - high.astype(F32)))
     each = jnp.concatenate([high.astype(F32), middle.astype(F32), low.astype(F32)], axis=0)
     each = jnp.broadcast_to(each[:, None, :], (3 * MAT, SUB, LANES)).reshape(3 * MAT * SUB, LANES)
@@ -124,6 +127,11 @@
     gain = wide_lanes(jnp.broadcast_to(gain_ref[...], (SUB, PORTS)), room)
     for p in range(PORTS):
         gains[p] = jnp.broadcast_to(gain[:, p : p + 1], (SUB, LANES))
+    from_lane = iota((LANES, LANES), 0) - iota((LANES, LANES), 1)
+    for j in range(2 * REACH):
+        shift = (from_lane == offset_of(j)).astype(BF16)
+        for s in range(2):
+            shifts[j // 2, s * LANES : (s + 1) * LANES, j % 2 * LANES : (j % 2 + 1) * LANES] = shift
     zero = jnp.zeros((SUB, LANES), F32)
     for x in range(REACH):
         for c in range(COLS):
@@ -136,27 +144,52 @@
             along_x[REACH + x, c] = v
             along_y[x, c, 0:SUB] = v
             along_y[x, c, SUB : 2 * SUB] = v
+        high, low = split(along_x[REACH + x].reshape(COLS * SUB, LANES))
+        at = pl.ds(pl.multiple_of(x * COLS * SUB, COLS * SUB), COLS * SUB)
+        own[at, :LANES] = high
+        own[at, LANES:] = low
         return carry
 
     lax.fori_loop(0, size_x, prepare, 0)
     for copy in loads:
         copy.wait()
 
-    def hot(x):
+    lines = size_x * SUB
+
+    def shift_all(n, carry):
+        for s in range(2):
+            part = slice(s * COLS * lines // 2, (s + 1) * COLS * lines // 2)
+            shifted[n, part] = plain_dot(own[part, :], shifts[n])
+        return carry
+
+    lax.fori_loop(0, REACH, shift_all, 0)
+
+    def hot(x, carry):
         kind = classes_ref[x]
         one = jnp.concatenate([(kind == m).astype(F32) for m in range(MAT)], axis=0).astype(BF16)
-        return jnp.concatenate([one, one, one], axis=0)
-
-    def plane(x, at):
+        hots[:, pl.ds(pl.multiple_of(x * LANES, LANES), LANES)] = jnp.concatenate([one, one, one], axis=0)
+        return carry
+
+    lax.fori_loop(0, size_x, hot, 0)
+
+    def coefficients(i, carry):
+        for s in range(2):
+            at = pl.ds(pl.multiple_of((2 * i + s) * 2 * LANES, 2 * LANES), 2 * LANES)
+            coefs[:, at] = plain_dot(spread[...], hots[:, at])
+        return carry
+
+    lax.fori_loop(0, size_x // 4, coefficients, 0)
+
+    def plane(x, carry):
         port = ports_ref[x]
-        coef_at = lambda t: coefs[t * SUB : (t + 1) * SUB, at * LANES : (at + 1) * LANES]
-        own = [along_x[REACH + x, c] for c in range(COLS)]
+        here = pl.ds(pl.multiple_of(x * LANES, LANES), LANES)
+        coef_at = lambda t: coefs[t * SUB : (t + 1) * SUB, here]
         diag = coef_at(6 * REACH)
         extra = zero
         for p in range(PORTS):
             extra = jnp.where(port == p + 1, gains[p], extra)
         diag = diag + extra
-        acc = [diag * v for v in own]
+        acc = [diag * along_x[REACH + x, c] for c in range(COLS)]
         for j in range(2 * REACH):
             coef = coef_at(j)
             for c in range(COLS):
@@ -172,35 +205,29 @@
             for c in range(COLS):
                 acc[c] = acc[c] - coef * along_y[x, c, k : k + SUB]
         for j in range(2 * REACH):
-            k = offset_of(j)
-            coef = jnp.where((lane + k >= 0) & (lane + k < LANES), coef_at(4 * REACH + j), 0.0)
-            for c in range(COLS):
-                acc[c] = acc[c] - coef * pltpu.roll(own[c], (-k) % LANES, 1)
+            coef = coef_at(4 * REACH + j)
+            for c in range(COLS):
+                line = pl.ds(pl.multiple_of((x * COLS + c) * SUB, SUB), SUB)
+                acc[c] = acc[c] - coef * shifted[j // 2, line, j % 2 * LANES : (j % 2 + 1) * LANES]
         for c in range(COLS):
             part_ref[x, c] = acc[c]
-
-    def pair(i, carry):
-        coefs[...] = plain_dot(spread[...], jnp.concatenate([hot(2 * i), hot(2 * i + 1)], axis=1))
-        plane(2 * i, 0)
-        plane(2 * i + 1, 1)
-        return carry
-
-    lax.fori_loop(0, size_x // 2, pair, 0)
-
-    load.wait()
-    wide = BLOCKS * COLS
-    lines = size_x * SUB
+        return carry
+
+    lax.fori_loop(0, size_x, plane, 0)
+
+    for copy in basis_loads:
+        copy.wait()
 
     def store(x, carry):
         for y in range(SUB):
-            high, low = split(whole[pl.ds(x * SUB + y, wide, stride=lines), :])
+            high, low = split(whole[x * SUB + y])
             at = pl.ds(pl.multiple_of((x * SUB + y) * LANES, LANES), LANES)
             both_ref[:, at] = jnp.concatenate([high, low], axis=0)
         return carry
 
     lax.fori_loop(0, size_x, store, 0)
-    both = both_ref[...]
-    products = rows_dot(both, both)
+    halves = [both_ref[:, : lines * LANES // 2], both_ref[:, lines * LANES // 2 :]]
+    products = sum(rows_dot(half, half) for half in halves)
     products = jnp.concatenate([products, jnp.zeros((2 * wide, LANES - 2 * wide), F32)], axis=1)
     products = products[:wide] + products[wide:]
     products = products + pltpu.roll(products, LANES - wide, 1)
@@ -213,12 +240,15 @@
 
 def halo_kernel(part_ref, coef_x_ref, coef_y_ref, both_ref, sums_ref,
                 xa_ref, xb_ref, ya_ref, yb_ref,
-                w_ref, out_ref, around, image, room):
+                w_ref, out_ref, around, outside, image, room):
     size_x = part_ref.shape[0]
     odd_x = odd_place(GX) == 1
     odd_y = odd_place(GY)
-    below_x = lambda p, c: jnp.where(odd_x, xa_ref[c, p], xb_ref[c, p])
-    above_x = lambda p, c: jnp.where(odd_x, xb_ref[c, p], xa_ref[c, p])
+    for p in range(REACH):
+        for c in range(COLS):
+            first, second = xa_ref[c, p], xb_ref[c, p]
+            outside[p, c] = jnp.where(odd_x, first, second)
+            outside[REACH + p, c] = jnp.where(odd_x, second, first)
     at_a = pl.ds(pl.multiple_of((1 - odd_y) * SUB, SUB), SUB)
     at_b = pl.ds(pl.multiple_of(odd_y * SUB, SUB), SUB)
     lines = size_x * SUB
@@ -237,7 +267,7 @@
                 continue
             coef = coef_x_ref[x, j % REACH]
             for c in range(COLS):
-                value = below_x(at + REACH, c) if at < 0 else above_x(at - size_x, c)
+                value = outside[at + REACH if at < 0 else at - size_x + REACH, c]
                 acc[c] = acc[c] - coef * value
         for c in range(COLS):
             image[c * lines + x * SUB : c * lines + (x + 1) * SUB, :] = acc[c]
@@ -245,13 +275,13 @@
             high, low = split(image[pl.ds(x * SUB + y, COLS, stride=lines), :])
             at = (x * SUB + y) * LANES
             w_ref[:, at : at + LANES] = jnp.concatenate([high, low], axis=0)
-    w = w_ref[...]
     wide = BLOCKS * COLS
+    halves = [slice(0, lines * LANES // 2), slice(lines * LANES // 2, lines * LANES)]
     lane = iota((SUB, LANES), 1)
-    q_w = wide_lanes(rows_dot(w, both_ref[...]), room)
+    q_w = wide_lanes(sum(rows_dot(w_ref[:, at], both_ref[:, at]) for at in halves), room)
     q_w = q_w[:COLS] + q_w[COLS:]
     q_w = jnp.where(lane < wide, q_w + pltpu.roll(q_w, LANES - wide, 1), 0.0)
-    w_w = wide_lanes(rows_dot(w, w), room)
+    w_w = wide_lanes(sum(rows_dot(w_ref[:, at], w_ref[:, at]) for at in halves), room)
     w_w = w_w[:COLS] + w_w[COLS:]
     w_w = jnp.where(lane < COLS, w_w + pltpu.roll(w_w, LANES - COLS, 1), 0.0)
     out_ref[...] = sums_ref[...] + pltpu.roll(q_w, QW_AT, 1) + pltpu.roll(w_w, WW_AT, 1)
@@ -269,7 +299,8 @@
 
 
 def finish_kernel(scale, taps_ref, received_ref, both_ref, w_ref,
-                  next_ref, projection_ref, triangle_ref, room, result, sems):
+                  next_ref, projection_ref, triangle_ref,
+                  room, result, sems, projection_room, triangle_room, small_sems):
     size_x = next_ref.shape[1] // SUB
     wide = BLOCKS * COLS
     row = iota((SUB, LANES), 0)
@@ -298,36 +329,49 @@
         + rows_dot(back_t, jnp.concatenate([inner, rest], axis=0), HIGHEST)
     )
     apply = jnp.where(lane == row + wide, 1.0, back_t)
-    for k in range(COLS):
-        column = jnp.broadcast_to(gram[:, k : k + 1], (SUB, LANES))
-        pivot = jnp.broadcast_to(gram[k : k + 1, k : k + 1], (SUB, LANES))
-        inverse = root_inverse(pivot)
-        gram_row = jnp.broadcast_to(gram[k : k + 1, :], (SUB, LANES)) * inverse
-        apply_row = jnp.broadcast_to(apply[k : k + 1, :], (SUB, LANES)) * inverse
-        factor = jnp.where(row > k, column * inverse, 0.0)
-        gram = jnp.where(row == k, gram_row, gram - factor * gram_row)
-        apply = jnp.where(row == k, apply_row, apply - factor * apply_row)
-    triangle_ref[...] = jnp.where(lane >= row, gram, 0.0)[:, :COLS]
-    projection_ref[...] = p_t[:, :wide]
+    every = lambda value: jnp.broadcast_to(value, (SUB, LANES))
+    for k in range(0, COLS, 2):
+        first, second = every(gram[:, k : k + 1]), every(gram[:, k + 1 : k + 2])
+        inverse = root_inverse(every(gram[k : k + 1, k : k + 1]))
+        beside = every(gram[k : k + 1, k + 1 : k + 2]) * inverse
+        inverse_next = root_inverse(every(gram[k + 1 : k + 2, k + 1 : k + 2]) - beside * beside)
+        first = first * inverse
+        second = (second - beside * first) * inverse_next
+        first = jnp.where(row > k + 1, first, 0.0)
+        second = jnp.where(row > k + 1, second, 0.0)
+
+        def step(value):
+            top = every(value[k : k + 1, :]) * inverse
+            low = (every(value[k + 1 : k + 2, :]) - beside * top) * inverse_next
+            value = value - first * top - second * low
+            return jnp.where(row == k, top, jnp.where(row == k + 1, low, value))
+
+        gram, apply = step(gram), step(apply)
+    triangle_room[...] = jnp.where(lane >= row, gram, 0.0)[:, :COLS]
+    projection_room[...] = p_t[:, :wide]
+    copies = [
+        pltpu.make_async_copy(triangle_room, triangle_ref, small_sems.at[0]),
+        pltpu.make_async_copy(projection_room, projection_ref, small_sems.at[1]),
+    ]
+    for copy in copies:
+        copy.start()
     high, low = split(apply)
     pieces = jnp.concatenate([high.astype(F32), low.astype(F32)], axis=0)
     lane = iota(pieces.shape, 1)
     on_both = jnp.where(lane < wide, pieces, pltpu.roll(pieces, wide, 1))[:, : 2 * wide].astype(BF16)
     pieces = pltpu.roll(pieces, LANES - wide, 1)
     on_w = jnp.where(lane < COLS, pieces, pltpu.roll(pieces, COLS, 1))[:, : 2 * COLS].astype(BF16)
-    lines = size_x * SUB
-    group = size_x // 4
-    copies = []
+    group = size_x // 8
     for x in range(size_x):
         at = slice(x * SUB * LANES, (x + 1) * SUB * LANES)
         block = plain_dot(on_both, both_ref[:, at]) + plain_dot(on_w, w_ref[:, at])
         block = block[:COLS] + block[COLS:]
         for y in range(SUB):
-            result[pl.ds(x * SUB + y, COLS, stride=lines), :] = block[:, y * LANES : (y + 1) * LANES]
+            result[x * SUB + y] = block[:, y * LANES : (y + 1) * LANES]
         if x % group == group - 1:
             for c in range(COLS):
                 copies.append(pltpu.make_async_copy(
-                    result.at[pl.ds(c * lines + (x + 1 - group) * SUB, group * SUB)],
+                    result.at[pl.ds((x + 1 - group) * SUB, group * SUB), c],
                     next_ref.at[c, pl.ds((x + 1 - group) * SUB, group * SUB)],
                     sems.at[x // group, c],
                 ))
@@ -380,16 +424,20 @@
             pltpu.VMEM((PORTS, SUB, LANES), F32),
             pltpu.VMEM((SUB, LANES), F32),
             pltpu.VMEM(((6 * REACH + 1) * SUB, 3 * MAT * SUB), BF16),
-            pltpu.VMEM(((6 * REACH + 1) * SUB, 2 * LANES), F32),
-            pltpu.VMEM((wide * lines, LANES), F32),
+            pltpu.VMEM((3 * MAT * SUB, size_x * LANES), BF16),
+            pltpu.VMEM(((6 * REACH + 1) * SUB, size_x * LANES), F32),
+            pltpu.VMEM((lines, wide, LANES), F32),
+            pltpu.VMEM((COLS * lines, 2 * LANES), BF16),
+            pltpu.VMEM((REACH, 2 * LANES, 2 * LANES), BF16),
+            pltpu.VMEM((REACH, COLS * lines, 2 * LANES), F32),
             pltpu.VMEM((size_x, SUB, LANES), jnp.int32),
             pltpu.VMEM((size_x, SUB, LANES), jnp.int32),
-            pltpu.SemaphoreType.DMA((3,)),
+            pltpu.SemaphoreType.DMA((2 + wide,)),
         ],
-        compiler_params=limit(16),
+        compiler_params=limit(26),
         cost_estimate=pl.CostEstimate(flops=10**9, bytes_accessed=8 * 2**20, transcendentals=0),
         name="local",
-    )(taps, port_gain[None], in_hbm(basis.reshape(wide * lines, LANES)), block, in_hbm(classes), in_hbm(ports))
+    )(taps, port_gain[None], in_hbm(basis.reshape(wide, lines, LANES)), block, in_hbm(classes), in_hbm(ports))
     w, sums = pl.pallas_call(
         halo_kernel,
         out_shape=(shape((2 * COLS, cells), BF16), tile),
@@ -397,6 +445,7 @@
         out_specs=(VMEM,) * 2,
         scratch_shapes=[
             pltpu.VMEM((size_x, COLS, 2 * SUB, LANES), F32),
+            pltpu.VMEM((2 * REACH, COLS, SUB, LANES), F32),
             pltpu.VMEM((COLS * lines, LANES), F32),
             pltpu.VMEM((2 * COLS, LANES), F32),
         ],
@@ -426,11 +475,14 @@
             shape((COLS, COLS), F32),
         ),
         in_specs=[VMEM] * 4,
-        out_specs=(HBM, VMEM, VMEM),
+        out_specs=(HBM, HBM, HBM),
         scratch_shapes=[
             pltpu.VMEM((MAT, LANES), F32),
-            pltpu.VMEM((COLS * lines, LANES), F32),
-            pltpu.SemaphoreType.DMA((4, COLS)),
+            pltpu.VMEM((lines, COLS, LANES), F32),
+            pltpu.SemaphoreType.DMA((8, COLS)),
+            pltpu.VMEM((COLS, wide), F32),
+            pltpu.VMEM((COLS, COLS), F32),
+            pltpu.SemaphoreType.DMA((2,)),
         ],
         compiler_params=limit(8),
         name="finish",

time: 80.4 us -> 79.8 us (level)
  waiting for transfers between devices: 2.3 us -> 1.08 us
    all_to_all x1, blocking collectives: 13.6 us -> 14.7 us  [per_device(): along_gx = lax.all_to_all(fold(lax.axis_size(GX), sums, beside), GX, 0, 0)]
    all_to_all x1, blocking collectives: 29 us -> 27.9 us  [per_device(): lax.all_to_all(fold(lax.axis_size('gy_0'), along_gx), 'gy_0', 0, 0)]
    pallas_call x1, Pallas kernels: 6.49 us -> 7.57 us  [per_device(): pl.pallas_call(local_kernel, out_shape=(shape((size_x, COLS, SUB, LANES),...]
    ppermute x1, waiting for transfers between devices: 1.16 us -> 0.08 us  [per_device(): xb = lax.ppermute(xb, GX, x_second)]
  transfers between devices with their start and end apart: 5 -> 5, of which waited for: 2 -> 2; matrix products, arithmetic and copies ran while one was open for 0% -> 0% of each run, Pallas kernels for 8% -> 10%
where the time goes in v2:
time: 79.8 us; the launch traced here: 79.4 us
  blocking collectives  42.6 us (53%)
  starting transfers between devices  21.6 us (27%)
  Pallas kernels  13.4 us (17%)
  waiting for transfers between devices  1.08 us (1%)
    all_to_all x1, blocking collectives, per_device(): lax.all_to_all(fold(lax.axis_size('gy_0'), along_gx), 'gy_0', 0, 0)  27.9 us
    all_to_all x1, blocking collectives, per_device(): along_gx = lax.all_to_all(fold(lax.axis_size(GX), sums, beside), GX, 0, 0)  14.7 us
    ppermute x1, starting transfers between devices, per_device(): xa = lax.ppermute(xa, GX, x_first)  11.3 us
    pallas_call x1, Pallas kernels, per_device(): pl.pallas_call(local_kernel, out_shape=(shape((size_x, COLS, SUB, LANES),...  7.57 us
    ppermute x1, starting transfers between devices, per_device(): ya = lax.ppermute(block, GY, y_first)  5.61 us
    pallas_call x1, Pallas kernels, per_device(): pl.pallas_call(functools.partial(finish_kernel, 1.0 / total), out_shape=(...  2.81 us
    ppermute x1, starting transfers between devices, per_device(): beside = lax.ppermute(sums, 'gy_1', [(0, 1), (1, 0)])  2.09 us
    ppermute x1, starting transfers between devices, per_device(): xb = lax.ppermute(xb, GX, x_second)  1.92 us
  transfers between devices with their start and end apart: 5, of which 2 were waited for; matrix products, arithmetic and copies ran while one was open for 0% of the time, Pallas kernels for 10%

profile of v2, /device:TPU:8, one launch (start us, length us, event | category | flops | bytes accessed | tf_op | source)
XLA Modules:
  0.0 79.4 jit_solution(13926512776163214586)
XLA Ops:
  0.6 0.0 copy-start
  0.6 0.0 copy-start.1
  0.7 1.2 %edges.1 = (f32[8,16,8,128]{3,2,1,0:T(8,128)S(1)}, f32[8,7,8,128]{3,2,1,0:T(8,128)S(1)}, f32[8,7,8,128]{3,2,1,0:T(8,128)S(1)}) custom-call(f32[32,16,8,128]{3,2,1,0:T(8,128)} %basis_ref.1), custom_call_target="tpu_custom_call" | custom-call | tf_op jit(solution)/shard_map/edges/pallas_call | solution.py:397
  1.9 0.7 collective-permute-start.3
  2.6 5.6 %collective-permute-start.2 = (f32[8,16,8,128]{3,2,1,0:T(8,128)S(1)}, f32[8,16,8,128]{3,2,1,0:T(8,128)S(1)}, u32[]{:S(2)}, u32[]{:S(2)}) collective-permute-start(f32[8,16,8,128]{3,2,1,0:T(8,128)S(1)} %get-tuple-element.16.block_ref), channel_id=1, source_target_pairs={{0,1},{1,0},{2,3},{3,2},{4,5},{5,4},{6,7},{7,6},{8,9},{9,8},{10,11... | collective-permute-start | bytes 1572872 | tf_op jit(solution)/shard_map/ppermute | solution.py:409
  8.2 11.3 %collective-permute-start = (f32[8,7,8,128]{3,2,1,0:T(8,128)S(1)}, f32[8,7,8,128]{3,2,1,0:T(8,128)S(1)}, u32[]{:S(2)}, u32[]{:S(2)}) collective-permute-start(f32[8,7,8,128]{3,2,1,0:T(8,128)S(1)} %get-tuple-element.22), channel_id=1, source_target_pairs={{0,32},{32,0},{64,96},{96,64},{128,160},{160,128},{192,224},{224,1... | collective-permute-start | bytes 688136 | tf_op jit(solution)/shard_map/ppermute | solution.py:408
  19.5 1.9 %collective-permute-start.1 = (f32[8,7,8,128]{3,2,1,0:T(8,128)S(1)}, f32[8,7,8,128]{3,2,1,0:T(8,128)S(1)}, u32[]{:S(2)}, u32[]{:S(2)}) collective-permute-start(f32[8,7,8,128]{3,2,1,0:T(8,128)S(1)} %get-tuple-element.23), channel_id=1, source_target_pairs={{32,64},{64,32},{96,128},{128,96},{160,192},{192,160},{224,256},{2... | collective-permute-start | bytes 688136 | tf_op jit(solution)/shard_map/ppermute | solution.py:407
  21.4 0.0 copy-done
  21.4 0.0 copy-done.1
  21.4 7.6 %local.1 = (f32[16,8,8,128]{3,2,1,0:T(8,128)S(1)}, f32[16,7,8,128]{3,2,1,0:T(8,128)S(1)}, f32[16,7,8,128]{3,2,1,0:T(8,128)S(1)}, bf16[64,16384]{1,0:T(8,128)(2,1)S(1)}, f32[8,128]{1,0:T(8,128)S(1)}) custom-call(f32[8,42]{1,0:T(8,128)S(1)} %copy-done, f32[1,8]{1,0:T(1,128)S(1)} %bitcast.4, f32[32,128,128]{2,1,0:T(8,128)} %bitcast.5, ...), custom_call_target="tpu_custom_call" | custom-call | flops 1000000000 | bytes 8388608 | tf_op jit(solution)/shard_map/local/pallas_call | solution.py:410
  29.0 0.0 collective-permute-done.xa_ref
  29.0 0.1 collective-permute-done.1.xb_ref
  29.1 0.0 collective-permute-done.3.yb_ref
  29.1 0.0 collective-permute-done.2.ya_ref
  29.1 1.8 %halo.1 = (bf16[16,16384]{1,0:T(8,128)(2,1)S(1)}, f32[8,128]{1,0:T(8,128)S(1)}) custom-call(f32[16,8,8,128]{3,2,1,0:T(8,128)S(1)} %get-tuple-element.17.part_ref, f32[16,7,8,128]{3,2,1,0:T(8,128)S(1)} %get-tuple-element.18.coef_x_ref, f32[16,7,8,128]{3,2,1,0:T(8,128)S(1)} %get-tuple-element.19.coef_y_ref, bf16[64,16384]{1,0:T(8,128)(2,1)S(1)} %get-tuple-element.20.both_ref, ...), custom_call_target="tpu_custom_call" | custom-call | tf_op jit(solution)/shard_map/halo/pallas_call | solution.py:441
  30.9 2.1 %collective-permute-start.4 = (f32[8,128]{1,0:T(8,128)S(1)}, f32[8,128]{1,0:T(8,128)S(1)}, u32[]{:S(2)}, u32[]{:S(2)}) collective-permute-start(f32[8,128]{1,0:T(8,128)S(1)} %get-tuple-element.24.refs_0_), channel_id=1, source_target_pairs={{0,1},{1,0},{2,3},{3,2},{4,5},{5,4},{6,7},{7,6},{8,9},{9,8},{10,11... | collective-permute-start | bytes 12296 | tf_op jit(solution)/shard_map/ppermute | solution.py:466
  33.0 1.0 %collective-permute-done.4.refs_1_ = f32[8,128]{1,0:T(8,128)S(1)} collective-permute-done((f32[8,128]{1,0:T(8,128)S(1)}, f32[8,128]{1,0:T(8,128)S(1)}, u32[]{:S(2)}, u32[]{:S(2)}) %collective-permute-start.4) | collective-permute-done | bytes 4128 | tf_op jit(solution)/shard_map/ppermute | solution.py:466
  34.0 14.7 %all_to_all.10.refs_0_ = f32[32,8,128]{2,1,0:T(8,128)S(1)} all-to-all(f32[32,8,128]{2,1,0:T(8,128)S(1)} %fold.2), channel_id=1, replica_groups=mesh['gx_0'=4,'gx_1'=8,'gy_0'=16,'gy_1'=2] {'gx_0','gx_1'}, dimensions={0} | all-to-all | bytes 262144 | tf_op jit(solution)/shard_map/all_to_all | solution.py:467
  48.8 27.9 %all_to_all.11.received_ref = f32[16,8,128]{2,1,0:T(8,128)S(1)} all-to-all(f32[16,8,128]{2,1,0:T(8,128)S(1)} %fold.3), channel_id=1, replica_groups=mesh['gx_0'=4,'gx_1'=8,'gy_0'=16,'gy_1'=2] {'gy_0'}, dimensions={0} | all-to-all | bytes 131072 | tf_op jit(solution)/shard_map/all_to_all | solution.py:468
  76.6 2.8 %finish.1 = (f32[8,128,128]{2,1,0:T(8,128)}, f32[8,32]{1,0:T(8,128)}, f32[8,8]{1,0:T(8,128)}) custom-call(f32[8,42]{1,0:T(8,128)S(1)} %copy-done, f32[16,8,128]{2,1,0:T(8,128)S(1)} %all_to_all.11.received_ref, bf16[64,16384]{1,0:T(8,128)(2,1)S(1)} %get-tuple-element.20.both_ref, bf16[16,16384]{1,0:T(8,128)(2,1)S(1)} %get-tuple-element.25.w_ref), custom_call_target="tpu_custom_call" | custom-call | tf_op jit(solution)/shard_map/finish/pallas_call | solution.py:470
  (2 shorter events, 0.0 us)
Async XLA Ops:
  0.6 20.8 %copy-start = (f32[8,42]{1,0:T(8,128)S(1)}, f32[8,42]{1,0:T(8,128)}, u32[]{:S(2)}) copy-start(f32[8,42]{1,0:T(8,128)} %taps_ref.3) | copy-start | bytes 4036
  0.6 20.8 %copy-start.1 = (f32[8]{0:T(128)S(1)}, f32[8]{0:T(128)}, u32[]{:S(2)}) copy-start(f32[8]{0:T(128)} %param.9) | copy-start | bytes 100
  1.9 27.2 %collective-permute-start.3 = (f32[8,16,8,128]{3,2,1,0:T(8,128)S(1)}, f32[8,16,8,128]{3,2,1,0:T(8,128)S(1)}, u32[]{:S(2)}, u32[]{:S(2)}) collective-permute-start(f32[8,16,8,128]{3,2,1,0:T(8,128)S(1)} %get-tuple-element.16.block_ref), channel_id=1, source_target_pairs={{1,2},{2,1},{3,4},{4,3},{5,6},{6,5},{7,8},{8,7},{9,10},{10,9},{11,... | collective-permute-start | bytes 1572872 | tf_op jit(solution)/shard_map/ppermute | solution.py:406
  2.6 26.5 %collective-permute-start.2 = (f32[8,16,8,128]{3,2,1,0:T(8,128)S(1)}, f32[8,16,8,128]{3,2,1,0:T(8,128)S(1)}, u32[]{:S(2)}, u32[]{:S(2)}) collective-permute-start(f32[8,16,8,128]{3,2,1,0:T(8,128)S(1)} %get-tuple-element.16.block_ref), channel_id=1, source_target_pairs={{0,1},{1,0},{2,3},{3,2},{4,5},{5,4},{6,7},{7,6},{8,9},{9,8},{10,11... | collective-permute-start | bytes 1572872 | tf_op jit(solution)/shard_map/ppermute | solution.py:409
  8.2 20.8 %collective-permute-start = (f32[8,7,8,128]{3,2,1,0:T(8,128)S(1)}, f32[8,7,8,128]{3,2,1,0:T(8,128)S(1)}, u32[]{:S(2)}, u32[]{:S(2)}) collective-permute-start(f32[8,7,8,128]{3,2,1,0:T(8,128)S(1)} %get-tuple-element.22), channel_id=1, source_target_pairs={{0,32},{32,0},{64,96},{96,64},{128,160},{160,128},{192,224},{224,1... | collective-permute-start | bytes 688136 | tf_op jit(solution)/shard_map/ppermute | solution.py:408
  19.5 9.6 %collective-permute-start.1 = (f32[8,7,8,128]{3,2,1,0:T(8,128)S(1)}, f32[8,7,8,128]{3,2,1,0:T(8,128)S(1)}, u32[]{:S(2)}, u32[]{:S(2)}) collective-permute-start(f32[8,7,8,128]{3,2,1,0:T(8,128)S(1)} %get-tuple-element.23), channel_id=1, source_target_pairs={{32,64},{64,32},{96,128},{128,96},{160,192},{192,160},{224,256},{2... | collective-permute-start | bytes 688136 | tf_op jit(solution)/shard_map/ppermute | solution.py:407
  30.9 3.1 %collective-permute-start.4 = (f32[8,128]{1,0:T(8,128)S(1)}, f32[8,128]{1,0:T(8,128)S(1)}, u32[]{:S(2)}, u32[]{:S(2)}) collective-permute-start(f32[8,128]{1,0:T(8,128)S(1)} %get-tuple-element.24.refs_0_), channel_id=1, source_target_pairs={{0,1},{1,0},{2,3},{3,2},{4,5},{5,4},{6,7},{7,6},{8,9},{9,8},{10,11... | collective-permute-start | bytes 12296 | tf_op jit(solution)/shard_map/ppermute | solution.py:466

commit v3 on v2

--- a/solution.py
+++ b/solution.py
@@ -101,7 +101,7 @@
 
 def local_kernel(taps_ref, gain_ref, basis_ref, block_ref, classes_hbm, ports_hbm,
                  part_ref, coef_x_ref, coef_y_ref, both_ref, sums_ref,
-                 along_x, along_y, gains, room, spread, hots, coefs, whole, own, shifts, shifted,
+                 along_x, along_y, gains, room, spread, coefs, whole,
                  classes_ref, ports_ref, sems):
     size_x = classes_ref.shape[0]
     wide = BLOCKS * COLS
@@ -127,11 +127,6 @@
     gain = wide_lanes(jnp.broadcast_to(gain_ref[...], (SUB, PORTS)), room)
     for p in range(PORTS):
         gains[p] = jnp.broadcast_to(gain[:, p : p + 1], (SUB, LANES))
-    from_lane = iota((LANES, LANES), 0) - iota((LANES, LANES), 1)
-    for j in range(2 * REACH):
-        shift = (from_lane == offset_of(j)).astype(BF16)
-        for s in range(2):
-            shifts[j // 2, s * LANES : (s + 1) * LANES, j % 2 * LANES : (j % 2 + 1) * LANES] = shift
     zero = jnp.zeros((SUB, LANES), F32)
     for x in range(REACH):
         for c in range(COLS):
@@ -144,10 +139,6 @@
             along_x[REACH + x, c] = v
             along_y[x, c, 0:SUB] = v
             along_y[x, c, SUB : 2 * SUB] = v
-        high, low = split(along_x[REACH + x].reshape(COLS * SUB, LANES))
-        at = pl.ds(pl.multiple_of(x * COLS * SUB, COLS * SUB), COLS * SUB)
-        own[at, :LANES] = high
-        own[at, LANES:] = low
         return carry
 
     lax.fori_loop(0, size_x, prepare, 0)
@@ -156,40 +147,24 @@
 
     lines = size_x * SUB
 
-    def shift_all(n, carry):
-        for s in range(2):
-            part = slice(s * COLS * lines // 2, (s + 1) * COLS * lines // 2)
-            shifted[n, part] = plain_dot(own[part, :], shifts[n])
-        return carry
-
-    lax.fori_loop(0, REACH, shift_all, 0)
-
-    def hot(x, carry):
+    def coefficients(x):
         kind = classes_ref[x]
         one = jnp.concatenate([(kind == m).astype(F32) for m in range(MAT)], axis=0).astype(BF16)
-        hots[:, pl.ds(pl.multiple_of(x * LANES, LANES), LANES)] = jnp.concatenate([one, one, one], axis=0)
-        return carry
-
-    lax.fori_loop(0, size_x, hot, 0)
-
-    def coefficients(i, carry):
-        for s in range(2):
-            at = pl.ds(pl.multiple_of((2 * i + s) * 2 * LANES, 2 * LANES), 2 * LANES)
-            coefs[:, at] = plain_dot(spread[...], hots[:, at])
-        return carry
-
-    lax.fori_loop(0, size_x // 4, coefficients, 0)
+        return plain_dot(spread[...], jnp.concatenate([one, one, one], axis=0))
+
+    coefs[...] = coefficients(0)
 
     def plane(x, carry):
         port = ports_ref[x]
-        here = pl.ds(pl.multiple_of(x * LANES, LANES), LANES)
-        coef_at = lambda t: coefs[t * SUB : (t + 1) * SUB, here]
+        own = [along_x[REACH + x, c] for c in range(COLS)]
+        later = coefficients(jnp.minimum(x + 1, size_x - 1))
+        coef_at = lambda t: coefs[t * SUB : (t + 1) * SUB, :]
         diag = coef_at(6 * REACH)
         extra = zero
         for p in range(PORTS):
             extra = jnp.where(port == p + 1, gains[p], extra)
         diag = diag + extra
-        acc = [diag * along_x[REACH + x, c] for c in range(COLS)]
+        acc = [diag * v for v in own]
         for j in range(2 * REACH):
             coef = coef_at(j)
             for c in range(COLS):
@@ -205,12 +180,13 @@
             for c in range(COLS):
                 acc[c] = acc[c] - coef * along_y[x, c, k : k + SUB]
         for j in range(2 * REACH):
-            coef = coef_at(4 * REACH + j)
-            for c in range(COLS):
-                line = pl.ds(pl.multiple_of((x * COLS + c) * SUB, SUB), SUB)
-                acc[c] = acc[c] - coef * shifted[j // 2, line, j % 2 * LANES : (j % 2 + 1) * LANES]
+            k = offset_of(j)
+            coef = jnp.where((lane + k >= 0) & (lane + k < LANES), coef_at(4 * REACH + j), 0.0)
+            for c in range(COLS):
+                acc[c] = acc[c] - coef * pltpu.roll(own[c], (-k) % LANES, 1)
         for c in range(COLS):
             part_ref[x, c] = acc[c]
+        coefs[...] = later
         return carry
 
     lax.fori_loop(0, size_x, plane, 0)
@@ -424,17 +400,13 @@
             pltpu.VMEM((PORTS, SUB, LANES), F32),
             pltpu.VMEM((SUB, LANES), F32),
             pltpu.VMEM(((6 * REACH + 1) * SUB, 3 * MAT * SUB), BF16),
-            pltpu.VMEM((3 * MAT * SUB, size_x * LANES), BF16),
-            pltpu.VMEM(((6 * REACH + 1) * SUB, size_x * LANES), F32),
+            pltpu.VMEM(((6 * REACH + 1) * SUB, LANES), F32),
             pltpu.VMEM((lines, wide, LANES), F32),
-            pltpu.VMEM((COLS * lines, 2 * LANES), BF16),
-            pltpu.VMEM((REACH, 2 * LANES, 2 * LANES), BF16),
-            pltpu.VMEM((REACH, COLS * lines, 2 * LANES), F32),
             pltpu.VMEM((size_x, SUB, LANES), jnp.int32),
             pltpu.VMEM((size_x, SUB, LANES), jnp.int32),
             pltpu.SemaphoreType.DMA((2 + wide,)),
         ],
-        compiler_params=limit(26),
+        compiler_params=limit(16),
         cost_estimate=pl.CostEstimate(flops=10**9, bytes_accessed=8 * 2**20, transcendentals=0),
         name="local",
     )(taps, port_gain[None], in_hbm(basis.reshape(wide, lines, LANES)), block, in_hbm(classes), in_hbm(ports))

time: 79.8 us -> 79.8 us (level)
  waiting for transfers between devices: 1.08 us -> 2.77 us
  Pallas kernels: 13.4 us -> 11.9 us
    ppermute x1, waiting for transfers between devices: 0.08 us -> 1.63 us  [per_device(): xb = lax.ppermute(xb, GX, x_second)]
    pallas_call x1, Pallas kernels: 7.57 us -> 6.03 us  [per_device(): pl.pallas_call(local_kernel, out_shape=(shape((size_x, COLS, SUB, LANES),...]
    all_to_all x1, blocking collectives: 14.7 us -> 13.3 us  [per_device(): along_gx = lax.all_to_all(fold(lax.axis_size(GX), sums, beside), GX, 0, 0)]
    all_to_all x1, blocking collectives: 27.9 us -> 29.3 us  [per_device(): lax.all_to_all(fold(lax.axis_size('gy_0'), along_gx), 'gy_0', 0, 0)]
  transfers between devices with their start and end apart: 5 -> 5, of which waited for: 2 -> 2; matrix products, arithmetic and copies ran while one was open for 0% -> 0% of each run, Pallas kernels for 10% -> 8%
where the time goes in v3:
time: 79.8 us; the launch traced here: 79.4 us
  blocking collectives  42.6 us (53%)
  starting transfers between devices  21.5 us (27%)
  Pallas kernels  11.9 us (15%)
  waiting for transfers between devices  2.77 us (3%)
    all_to_all x1, blocking collectives, per_device(): lax.all_to_all(fold(lax.axis_size('gy_0'), along_gx), 'gy_0', 0, 0)  29.3 us
    all_to_all x1, blocking collectives, per_device(): along_gx = lax.all_to_all(fold(lax.axis_size(GX), sums, beside), GX, 0, 0)  13.3 us
    ppermute x1, starting transfers between devices, per_device(): xa = lax.ppermute(xa, GX, x_first)  11.3 us
    pallas_call x1, Pallas kernels, per_device(): pl.pallas_call(local_kernel, out_shape=(shape((size_x, COLS, SUB, LANES),...  6.03 us
    ppermute x1, starting transfers between devices, per_device(): ya = lax.ppermute(block, GY, y_first)  5.61 us
    pallas_call x1, Pallas kernels, per_device(): pl.pallas_call(functools.partial(finish_kernel, 1.0 / total), out_shape=(...  2.81 us
    ppermute x1, starting transfers between devices, per_device(): beside = lax.ppermute(sums, 'gy_1', [(0, 1), (1, 0)])  1.94 us
    ppermute x1, starting transfers between devices, per_device(): xb = lax.ppermute(xb, GX, x_second)  1.92 us
  transfers between devices with their start and end apart: 5, of which 2 were waited for; matrix products, arithmetic and copies ran while one was open for 0% of the time, Pallas kernels for 8%

profile of v3, /device:TPU:8, one launch (start us, length us, event | category | flops | bytes accessed | tf_op | source)
XLA Modules:
  0.0 79.4 jit_solution(17541085991412711750)
XLA Ops:
  0.6 0.0 copy-start
  0.6 0.0 copy-start.1
  0.7 1.2 %edges.1 = (f32[8,16,8,128]{3,2,1,0:T(8,128)S(1)}, f32[8,7,8,128]{3,2,1,0:T(8,128)S(1)}, f32[8,7,8,128]{3,2,1,0:T(8,128)S(1)}) custom-call(f32[32,16,8,128]{3,2,1,0:T(8,128)} %basis_ref.1), custom_call_target="tpu_custom_call" | custom-call | tf_op jit(solution)/shard_map/edges/pallas_call | solution.py:373
  1.9 0.7 collective-permute-start.3
  2.6 5.6 %collective-permute-start.2 = (f32[8,16,8,128]{3,2,1,0:T(8,128)S(1)}, f32[8,16,8,128]{3,2,1,0:T(8,128)S(1)}, u32[]{:S(2)}, u32[]{:S(2)}) collective-permute-start(f32[8,16,8,128]{3,2,1,0:T(8,128)S(1)} %get-tuple-element.16.block_ref), channel_id=1, source_target_pairs={{0,1},{1,0},{2,3},{3,2},{4,5},{5,4},{6,7},{7,6},{8,9},{9,8},{10,11... | collective-permute-start | bytes 1572872 | tf_op jit(solution)/shard_map/ppermute | solution.py:385
  8.2 11.3 %collective-permute-start = (f32[8,7,8,128]{3,2,1,0:T(8,128)S(1)}, f32[8,7,8,128]{3,2,1,0:T(8,128)S(1)}, u32[]{:S(2)}, u32[]{:S(2)}) collective-permute-start(f32[8,7,8,128]{3,2,1,0:T(8,128)S(1)} %get-tuple-element.22), channel_id=1, source_target_pairs={{0,32},{32,0},{64,96},{96,64},{128,160},{160,128},{192,224},{224,1... | collective-permute-start | bytes 688136 | tf_op jit(solution)/shard_map/ppermute | solution.py:384
  19.5 1.9 %collective-permute-start.1 = (f32[8,7,8,128]{3,2,1,0:T(8,128)S(1)}, f32[8,7,8,128]{3,2,1,0:T(8,128)S(1)}, u32[]{:S(2)}, u32[]{:S(2)}) collective-permute-start(f32[8,7,8,128]{3,2,1,0:T(8,128)S(1)} %get-tuple-element.23), channel_id=1, source_target_pairs={{32,64},{64,32},{96,128},{128,96},{160,192},{192,160},{224,256},{2... | collective-permute-start | bytes 688136 | tf_op jit(solution)/shard_map/ppermute | solution.py:383
  21.4 0.0 copy-done
  21.4 0.0 copy-done.1
  21.4 6.0 %local.1 = (f32[16,8,8,128]{3,2,1,0:T(8,128)S(1)}, f32[16,7,8,128]{3,2,1,0:T(8,128)S(1)}, f32[16,7,8,128]{3,2,1,0:T(8,128)S(1)}, bf16[64,16384]{1,0:T(8,128)(2,1)S(1)}, f32[8,128]{1,0:T(8,128)S(1)}) custom-call(f32[8,42]{1,0:T(8,128)S(1)} %copy-done, f32[1,8]{1,0:T(1,128)S(1)} %bitcast.4, f32[32,128,128]{2,1,0:T(8,128)} %bitcast.5, ...), custom_call_target="tpu_custom_call" | custom-call | flops 1000000000 | bytes 8388608 | tf_op jit(solution)/shard_map/local/pallas_call | solution.py:386
  27.5 0.0 collective-permute-done.xa_ref
  27.5 1.6 %collective-permute-done.1.xb_ref = f32[8,7,8,128]{3,2,1,0:T(8,128)S(1)} collective-permute-done((f32[8,7,8,128]{3,2,1,0:T(8,128)S(1)}, f32[8,7,8,128]{3,2,1,0:T(8,128)S(1)}, u32[]{:S(2)}, u32[]{:S(2)}) %collective-permute-start.1) | collective-permute-done | bytes 229408 | tf_op jit(solution)/shard_map/ppermute | solution.py:383
  29.1 0.0 collective-permute-done.3.yb_ref
  29.1 0.0 collective-permute-done.2.ya_ref
  29.1 1.8 %halo.1 = (bf16[16,16384]{1,0:T(8,128)(2,1)S(1)}, f32[8,128]{1,0:T(8,128)S(1)}) custom-call(f32[16,8,8,128]{3,2,1,0:T(8,128)S(1)} %get-tuple-element.17.part_ref, f32[16,7,8,128]{3,2,1,0:T(8,128)S(1)} %get-tuple-element.18.coef_x_ref, f32[16,7,8,128]{3,2,1,0:T(8,128)S(1)} %get-tuple-element.19.coef_y_ref, bf16[64,16384]{1,0:T(8,128)(2,1)S(1)} %get-tuple-element.20.both_ref, ...), custom_call_target="tpu_custom_call" | custom-call | tf_op jit(solution)/shard_map/halo/pallas_call | solution.py:413
  30.9 1.9 %collective-permute-start.4 = (f32[8,128]{1,0:T(8,128)S(1)}, f32[8,128]{1,0:T(8,128)S(1)}, u32[]{:S(2)}, u32[]{:S(2)}) collective-permute-start(f32[8,128]{1,0:T(8,128)S(1)} %get-tuple-element.24.refs_0_), channel_id=1, source_target_pairs={{0,1},{1,0},{2,3},{3,2},{4,5},{5,4},{6,7},{7,6},{8,9},{9,8},{10,11... | collective-permute-start | bytes 12296 | tf_op jit(solution)/shard_map/ppermute | solution.py:438
  32.9 1.1 %collective-permute-done.4.refs_1_ = f32[8,128]{1,0:T(8,128)S(1)} collective-permute-done((f32[8,128]{1,0:T(8,128)S(1)}, f32[8,128]{1,0:T(8,128)S(1)}, u32[]{:S(2)}, u32[]{:S(2)}) %collective-permute-start.4) | collective-permute-done | bytes 4128 | tf_op jit(solution)/shard_map/ppermute | solution.py:438
  34.0 13.3 %all_to_all.10.refs_0_ = f32[32,8,128]{2,1,0:T(8,128)S(1)} all-to-all(f32[32,8,128]{2,1,0:T(8,128)S(1)} %fold.2), channel_id=1, replica_groups=mesh['gx_0'=4,'gx_1'=8,'gy_0'=16,'gy_1'=2] {'gx_0','gx_1'}, dimensions={0} | all-to-all | bytes 262144 | tf_op jit(solution)/shard_map/all_to_all | solution.py:439
  47.3 29.3 %all_to_all.11.received_ref = f32[16,8,128]{2,1,0:T(8,128)S(1)} all-to-all(f32[16,8,128]{2,1,0:T(8,128)S(1)} %fold.3), channel_id=1, replica_groups=mesh['gx_0'=4,'gx_1'=8,'gy_0'=16,'gy_1'=2] {'gy_0'}, dimensions={0} | all-to-all | bytes 131072 | tf_op jit(solution)/shard_map/all_to_all | solution.py:440
  76.6 2.8 %finish.1 = (f32[8,128,128]{2,1,0:T(8,128)}, f32[8,32]{1,0:T(8,128)}, f32[8,8]{1,0:T(8,128)}) custom-call(f32[8,42]{1,0:T(8,128)S(1)} %copy-done, f32[16,8,128]{2,1,0:T(8,128)S(1)} %all_to_all.11.received_ref, bf16[64,16384]{1,0:T(8,128)(2,1)S(1)} %get-tuple-element.20.both_ref, bf16[16,16384]{1,0:T(8,128)(2,1)S(1)} %get-tuple-element.25.w_ref), custom_call_target="tpu_custom_call" | custom-call | tf_op jit(solution)/shard_map/finish/pallas_call | solution.py:442
  (2 shorter events, 0.0 us)
Async XLA Ops:
  0.6 20.8 %copy-start = (f32[8,42]{1,0:T(8,128)S(1)}, f32[8,42]{1,0:T(8,128)}, u32[]{:S(2)}) copy-start(f32[8,42]{1,0:T(8,128)} %taps_ref.3) | copy-start | bytes 4036
  0.6 20.8 %copy-start.1 = (f32[8]{0:T(128)S(1)}, f32[8]{0:T(128)}, u32[]{:S(2)}) copy-start(f32[8]{0:T(128)} %param.9) | copy-start | bytes 100
  1.9 27.2 %collective-permute-start.3 = (f32[8,16,8,128]{3,2,1,0:T(8,128)S(1)}, f32[8,16,8,128]{3,2,1,0:T(8,128)S(1)}, u32[]{:S(2)}, u32[]{:S(2)}) collective-permute-start(f32[8,16,8,128]{3,2,1,0:T(8,128)S(1)} %get-tuple-element.16.block_ref), channel_id=1, source_target_pairs={{1,2},{2,1},{3,4},{4,3},{5,6},{6,5},{7,8},{8,7},{9,10},{10,9},{11,... | collective-permute-start | bytes 1572872 | tf_op jit(solution)/shard_map/ppermute | solution.py:382
  2.6 26.5 %collective-permute-start.2 = (f32[8,16,8,128]{3,2,1,0:T(8,128)S(1)}, f32[8,16,8,128]{3,2,1,0:T(8,128)S(1)}, u32[]{:S(2)}, u32[]{:S(2)}) collective-permute-start(f32[8,16,8,128]{3,2,1,0:T(8,128)S(1)} %get-tuple-element.16.block_ref), channel_id=1, source_target_pairs={{0,1},{1,0},{2,3},{3,2},{4,5},{5,4},{6,7},{7,6},{8,9},{9,8},{10,11... | collective-permute-start | bytes 1572872 | tf_op jit(solution)/shard_map/ppermute | solution.py:385
  8.2 19.3 %collective-permute-start = (f32[8,7,8,128]{3,2,1,0:T(8,128)S(1)}, f32[8,7,8,128]{3,2,1,0:T(8,128)S(1)}, u32[]{:S(2)}, u32[]{:S(2)}) collective-permute-start(f32[8,7,8,128]{3,2,1,0:T(8,128)S(1)} %get-tuple-element.22), channel_id=1, source_target_pairs={{0,32},{32,0},{64,96},{96,64},{128,160},{160,128},{192,224},{224,1... | collective-permute-start | bytes 688136 | tf_op jit(solution)/shard_map/ppermute | solution.py:384
  19.5 9.6 %collective-permute-start.1 = (f32[8,7,8,128]{3,2,1,0:T(8,128)S(1)}, f32[8,7,8,128]{3,2,1,0:T(8,128)S(1)}, u32[]{:S(2)}, u32[]{:S(2)}) collective-permute-start(f32[8,7,8,128]{3,2,1,0:T(8,128)S(1)} %get-tuple-element.23), channel_id=1, source_target_pairs={{32,64},{64,32},{96,128},{128,96},{160,192},{192,160},{224,256},{2... | collective-permute-start | bytes 688136 | tf_op jit(solution)/shard_map/ppermute | solution.py:383
  30.9 3.1 %collective-permute-start.4 = (f32[8,128]{1,0:T(8,128)S(1)}, f32[8,128]{1,0:T(8,128)S(1)}, u32[]{:S(2)}, u32[]{:S(2)}) collective-permute-start(f32[8,128]{1,0:T(8,128)S(1)} %get-tuple-element.24.refs_0_), channel_id=1, source_target_pairs={{0,1},{1,0},{2,3},{3,2},{4,5},{5,4},{6,7},{7,6},{8,9},{9,8},{10,11... | collective-permute-start | bytes 12296 | tf_op jit(solution)/shard_map/ppermute | solution.py:438

commit v4 on v3

--- a/solution.py
+++ b/solution.py
@@ -189,7 +189,7 @@
         coefs[...] = later
         return carry
 
-    lax.fori_loop(0, size_x, plane, 0)
+    lax.fori_loop(0, size_x, plane, 0, unroll=2)
 
     for copy in basis_loads:
         copy.wait()
@@ -216,7 +216,7 @@
 
 def halo_kernel(part_ref, coef_x_ref, coef_y_ref, both_ref, sums_ref,
                 xa_ref, xb_ref, ya_ref, yb_ref,
-                w_ref, out_ref, around, outside, image, room):
+                w_ref, out_ref, around, outside, room):
     size_x = part_ref.shape[0]
     odd_x = odd_place(GX) == 1
     odd_y = odd_place(GY)
@@ -245,10 +245,9 @@
             for c in range(COLS):
                 value = outside[at + REACH if at < 0 else at - size_x + REACH, c]
                 acc[c] = acc[c] - coef * value
-        for c in range(COLS):
-            image[c * lines + x * SUB : c * lines + (x + 1) * SUB, :] = acc[c]
+        by_line = jnp.swapaxes(jnp.stack(acc), 0, 1)
         for y in range(SUB):
-            high, low = split(image[pl.ds(x * SUB + y, COLS, stride=lines), :])
+            high, low = split(by_line[y])
             at = (x * SUB + y) * LANES
             w_ref[:, at : at + LANES] = jnp.concatenate([high, low], axis=0)
     wide = BLOCKS * COLS
@@ -418,7 +417,6 @@
         scratch_shapes=[
             pltpu.VMEM((size_x, COLS, 2 * SUB, LANES), F32),
             pltpu.VMEM((2 * REACH, COLS, SUB, LANES), F32),
-            pltpu.VMEM((COLS * lines, LANES), F32),
             pltpu.VMEM((2 * COLS, LANES), F32),
         ],
         compiler_params=limit(8),

time: 79.8 us -> 79.6 us (level)
  transfers between devices with their start and end apart: 5 -> 5, of which waited for: 2 -> 2; matrix products, arithmetic and copies ran while one was open for 0% -> 0% of each run, Pallas kernels for 8% -> 7%
where the time goes in v4:
time: 79.6 us; the launch traced here: 79.3 us
  blocking collectives  42.6 us (54%)
  starting transfers between devices  21.5 us (27%)
  Pallas kernels  11.3 us (14%)
  waiting for transfers between devices  3.16 us (4%)
    all_to_all x1, blocking collectives, per_device(): lax.all_to_all(fold(lax.axis_size('gy_0'), along_gx), 'gy_0', 0, 0)  29.3 us
    all_to_all x1, blocking collectives, per_device(): along_gx = lax.all_to_all(fold(lax.axis_size(GX), sums, beside), GX, 0, 0)  13.3 us
    ppermute x1, starting transfers between devices, per_device(): xa = lax.ppermute(xa, GX, x_first)  11.3 us
    pallas_call x1, Pallas kernels, per_device(): pl.pallas_call(local_kernel, out_shape=(shape((size_x, COLS, SUB, LANES),...  5.63 us
    ppermute x1, starting transfers between devices, per_device(): ya = lax.ppermute(block, GY, y_first)  5.61 us
    pallas_call x1, Pallas kernels, per_device(): pl.pallas_call(functools.partial(finish_kernel, 1.0 / total), out_shape=(...  2.81 us
    ppermute x1, waiting for transfers between devices, per_device(): xb = lax.ppermute(xb, GX, x_second)  2.02 us
    ppermute x1, starting transfers between devices, per_device(): beside = lax.ppermute(sums, 'gy_1', [(0, 1), (1, 0)])  1.94 us
  transfers between devices with their start and end apart: 5, of which 2 were waited for; matrix products, arithmetic and copies ran while one was open for 0% of the time, Pallas kernels for 7%

profile of v4, /device:TPU:8, one launch (start us, length us, event | category | flops | bytes accessed | tf_op | source)
XLA Modules:
  0.0 79.3 jit_solution(18243429030427747309)
XLA Ops:
  0.6 0.0 copy-start
  0.6 0.0 copy-start.1
  0.7 1.2 %edges.1 = (f32[8,16,8,128]{3,2,1,0:T(8,128)S(1)}, f32[8,7,8,128]{3,2,1,0:T(8,128)S(1)}, f32[8,7,8,128]{3,2,1,0:T(8,128)S(1)}) custom-call(f32[32,16,8,128]{3,2,1,0:T(8,128)} %basis_ref.1), custom_call_target="tpu_custom_call" | custom-call | tf_op jit(solution)/shard_map/edges/pallas_call | solution.py:372
  1.9 0.7 collective-permute-start.3
  2.6 5.6 %collective-permute-start.2 = (f32[8,16,8,128]{3,2,1,0:T(8,128)S(1)}, f32[8,16,8,128]{3,2,1,0:T(8,128)S(1)}, u32[]{:S(2)}, u32[]{:S(2)}) collective-permute-start(f32[8,16,8,128]{3,2,1,0:T(8,128)S(1)} %get-tuple-element.16.block_ref), channel_id=1, source_target_pairs={{0,1},{1,0},{2,3},{3,2},{4,5},{5,4},{6,7},{7,6},{8,9},{9,8},{10,11... | collective-permute-start | bytes 1572872 | tf_op jit(solution)/shard_map/ppermute | solution.py:384
  8.2 11.3 %collective-permute-start = (f32[8,7,8,128]{3,2,1,0:T(8,128)S(1)}, f32[8,7,8,128]{3,2,1,0:T(8,128)S(1)}, u32[]{:S(2)}, u32[]{:S(2)}) collective-permute-start(f32[8,7,8,128]{3,2,1,0:T(8,128)S(1)} %get-tuple-element.22), channel_id=1, source_target_pairs={{0,32},{32,0},{64,96},{96,64},{128,160},{160,128},{192,224},{224,1... | collective-permute-start | bytes 688136 | tf_op jit(solution)/shard_map/ppermute | solution.py:383
  19.5 1.9 %collective-permute-start.1 = (f32[8,7,8,128]{3,2,1,0:T(8,128)S(1)}, f32[8,7,8,128]{3,2,1,0:T(8,128)S(1)}, u32[]{:S(2)}, u32[]{:S(2)}) collective-permute-start(f32[8,7,8,128]{3,2,1,0:T(8,128)S(1)} %get-tuple-element.23), channel_id=1, source_target_pairs={{32,64},{64,32},{96,128},{128,96},{160,192},{192,160},{224,256},{2... | collective-permute-start | bytes 688136 | tf_op jit(solution)/shard_map/ppermute | solution.py:382
  21.4 0.0 copy-done
  21.4 0.0 copy-done.1
  21.4 5.6 %local.1 = (f32[16,8,8,128]{3,2,1,0:T(8,128)S(1)}, f32[16,7,8,128]{3,2,1,0:T(8,128)S(1)}, f32[16,7,8,128]{3,2,1,0:T(8,128)S(1)}, bf16[64,16384]{1,0:T(8,128)(2,1)S(1)}, f32[8,128]{1,0:T(8,128)S(1)}) custom-call(f32[8,42]{1,0:T(8,128)S(1)} %copy-done, f32[1,8]{1,0:T(1,128)S(1)} %bitcast.4, f32[32,128,128]{2,1,0:T(8,128)} %bitcast.5, ...), custom_call_target="tpu_custom_call" | custom-call | flops 1000000000 | bytes 8388608 | tf_op jit(solution)/shard_map/local/pallas_call | solution.py:385
  27.1 0.0 collective-permute-done.xa_ref
  27.1 2.0 %collective-permute-done.1.xb_ref = f32[8,7,8,128]{3,2,1,0:T(8,128)S(1)} collective-permute-done((f32[8,7,8,128]{3,2,1,0:T(8,128)S(1)}, f32[8,7,8,128]{3,2,1,0:T(8,128)S(1)}, u32[]{:S(2)}, u32[]{:S(2)}) %collective-permute-start.1) | collective-permute-done | bytes 229408 | tf_op jit(solution)/shard_map/ppermute | solution.py:382
  29.1 0.0 collective-permute-done.3.yb_ref
  29.1 0.0 collective-permute-done.2.ya_ref
  29.1 1.7 %halo.1 = (bf16[16,16384]{1,0:T(8,128)(2,1)S(1)}, f32[8,128]{1,0:T(8,128)S(1)}) custom-call(f32[16,8,8,128]{3,2,1,0:T(8,128)S(1)} %get-tuple-element.17.part_ref, f32[16,7,8,128]{3,2,1,0:T(8,128)S(1)} %get-tuple-element.18.coef_x_ref, f32[16,7,8,128]{3,2,1,0:T(8,128)S(1)} %get-tuple-element.19.coef_y_ref, bf16[64,16384]{1,0:T(8,128)(2,1)S(1)} %get-tuple-element.20.both_ref, ...), custom_call_target="tpu_custom_call" | custom-call | tf_op jit(solution)/shard_map/halo/pallas_call | solution.py:412
  30.8 1.9 %collective-permute-start.4 = (f32[8,128]{1,0:T(8,128)S(1)}, f32[8,128]{1,0:T(8,128)S(1)}, u32[]{:S(2)}, u32[]{:S(2)}) collective-permute-start(f32[8,128]{1,0:T(8,128)S(1)} %get-tuple-element.24.refs_0_), channel_id=1, source_target_pairs={{0,1},{1,0},{2,3},{3,2},{4,5},{5,4},{6,7},{7,6},{8,9},{9,8},{10,11... | collective-permute-start | bytes 12296 | tf_op jit(solution)/shard_map/ppermute | solution.py:436
  32.7 1.1 %collective-permute-done.4.refs_1_ = f32[8,128]{1,0:T(8,128)S(1)} collective-permute-done((f32[8,128]{1,0:T(8,128)S(1)}, f32[8,128]{1,0:T(8,128)S(1)}, u32[]{:S(2)}, u32[]{:S(2)}) %collective-permute-start.4) | collective-permute-done | bytes 4128 | tf_op jit(solution)/shard_map/ppermute | solution.py:436
  33.9 13.3 %all_to_all.10.refs_0_ = f32[32,8,128]{2,1,0:T(8,128)S(1)} all-to-all(f32[32,8,128]{2,1,0:T(8,128)S(1)} %fold.2), channel_id=1, replica_groups=mesh['gx_0'=4,'gx_1'=8,'gy_0'=16,'gy_1'=2] {'gx_0','gx_1'}, dimensions={0} | all-to-all | bytes 262144 | tf_op jit(solution)/shard_map/all_to_all | solution.py:437
  47.2 29.3 %all_to_all.11.received_ref = f32[16,8,128]{2,1,0:T(8,128)S(1)} all-to-all(f32[16,8,128]{2,1,0:T(8,128)S(1)} %fold.3), channel_id=1, replica_groups=mesh['gx_0'=4,'gx_1'=8,'gy_0'=16,'gy_1'=2] {'gy_0'}, dimensions={0} | all-to-all | bytes 131072 | tf_op jit(solution)/shard_map/all_to_all | solution.py:438
  76.5 2.8 %finish.1 = (f32[8,128,128]{2,1,0:T(8,128)}, f32[8,32]{1,0:T(8,128)}, f32[8,8]{1,0:T(8,128)}) custom-call(f32[8,42]{1,0:T(8,128)S(1)} %copy-done, f32[16,8,128]{2,1,0:T(8,128)S(1)} %all_to_all.11.received_ref, bf16[64,16384]{1,0:T(8,128)(2,1)S(1)} %get-tuple-element.20.both_ref, bf16[16,16384]{1,0:T(8,128)(2,1)S(1)} %get-tuple-element.25.w_ref), custom_call_target="tpu_custom_call" | custom-call | tf_op jit(solution)/shard_map/finish/pallas_call | solution.py:440
  (2 shorter events, 0.0 us)
Async XLA Ops:
  0.6 20.8 %copy-start = (f32[8,42]{1,0:T(8,128)S(1)}, f32[8,42]{1,0:T(8,128)}, u32[]{:S(2)}) copy-start(f32[8,42]{1,0:T(8,128)} %taps_ref.3) | copy-start | bytes 4036
  0.6 20.8 %copy-start.1 = (f32[8]{0:T(128)S(1)}, f32[8]{0:T(128)}, u32[]{:S(2)}) copy-start(f32[8]{0:T(128)} %param.9) | copy-start | bytes 100
  1.9 27.2 %collective-permute-start.3 = (f32[8,16,8,128]{3,2,1,0:T(8,128)S(1)}, f32[8,16,8,128]{3,2,1,0:T(8,128)S(1)}, u32[]{:S(2)}, u32[]{:S(2)}) collective-permute-start(f32[8,16,8,128]{3,2,1,0:T(8,128)S(1)} %get-tuple-element.16.block_ref), channel_id=1, source_target_pairs={{1,2},{2,1},{3,4},{4,3},{5,6},{6,5},{7,8},{8,7},{9,10},{10,9},{11,... | collective-permute-start | bytes 1572872 | tf_op jit(solution)/shard_map/ppermute | solution.py:381
  2.6 26.5 %collective-permute-start.2 = (f32[8,16,8,128]{3,2,1,0:T(8,128)S(1)}, f32[8,16,8,128]{3,2,1,0:T(8,128)S(1)}, u32[]{:S(2)}, u32[]{:S(2)}) collective-permute-start(f32[8,16,8,128]{3,2,1,0:T(8,128)S(1)} %get-tuple-element.16.block_ref), channel_id=1, source_target_pairs={{0,1},{1,0},{2,3},{3,2},{4,5},{5,4},{6,7},{7,6},{8,9},{9,8},{10,11... | collective-permute-start | bytes 1572872 | tf_op jit(solution)/shard_map/ppermute | solution.py:384
  8.2 18.9 %collective-permute-start = (f32[8,7,8,128]{3,2,1,0:T(8,128)S(1)}, f32[8,7,8,128]{3,2,1,0:T(8,128)S(1)}, u32[]{:S(2)}, u32[]{:S(2)}) collective-permute-start(f32[8,7,8,128]{3,2,1,0:T(8,128)S(1)} %get-tuple-element.22), channel_id=1, source_target_pairs={{0,32},{32,0},{64,96},{96,64},{128,160},{160,128},{192,224},{224,1... | collective-permute-start | bytes 688136 | tf_op jit(solution)/shard_map/ppermute | solution.py:383
  19.5 9.6 %collective-permute-start.1 = (f32[8,7,8,128]{3,2,1,0:T(8,128)S(1)}, f32[8,7,8,128]{3,2,1,0:T(8,128)S(1)}, u32[]{:S(2)}, u32[]{:S(2)}) collective-permute-start(f32[8,7,8,128]{3,2,1,0:T(8,128)S(1)} %get-tuple-element.23), channel_id=1, source_target_pairs={{32,64},{64,32},{96,128},{128,96},{160,192},{192,160},{224,256},{2... | collective-permute-start | bytes 688136 | tf_op jit(solution)/shard_map/ppermute | solution.py:382
  30.8 3.1 %collective-permute-start.4 = (f32[8,128]{1,0:T(8,128)S(1)}, f32[8,128]{1,0:T(8,128)S(1)}, u32[]{:S(2)}, u32[]{:S(2)}) collective-permute-start(f32[8,128]{1,0:T(8,128)S(1)} %get-tuple-element.24.refs_0_), channel_id=1, source_target_pairs={{0,1},{1,0},{2,3},{3,2},{4,5},{5,4},{6,7},{7,6},{8,9},{9,8},{10,11... | collective-permute-start | bytes 12296 | tf_op jit(solution)/shard_map/ppermute | solution.py:436
